TPU v7x, 32 devices: a whole 2x2x4 slice. The times are simulated.
32 devices in a mesh: edge: 8 (over z, x), chan: 4 (over y, core).
Axes of the slice: x: 2, y: 2, z: 4, core: 2. Of those that a mesh axis runs over, the one named last changes fastest.
Arguments:
- edge_emb: bfloat16 [32768, 512], P('edge', 'chan'), may hold values from -6 to 6
- atom_emb: bfloat16 [1024, 256], P('edge'), may hold values from -6 to 6
- radial: bfloat16 [32768, 128], P('edge'), may hold values from 0 to 1
- circular: bfloat16 [16, 16, 32768], P(None, None, 'edge'), may hold values from -6 to 6
- spherical: bfloat16 [32, 8, 32768], P(None, None, 'edge'), may hold values from -6 to 6
- atom_tags: int32 [1024], P('edge'), may hold values from 0 to 2
- edge_source: int32 [32768], P('edge'), may hold values from 0 to 1023, as said below
- edge_target: int32 [32768], P('edge'), may hold values from 0 to 1023, as said below
- trip_source: int32 [16, 32768], P(None, 'edge'), may hold values from 0 to 12287, as said below
- trip_mask: int32 [16, 32768], P(None, 'edge'), may hold values from 0 to 1
- quad_source: int32 [8, 32768], P(None, 'edge'), may hold values from 0 to 12287, as said below
- quad_mask: int32 [8, 32768], P(None, 'edge'), may hold values from 0 to 1
- triplet_down_weight: bfloat16 [512, 64], P(None, 'chan'), may hold values from -0.25 to 0.25
- trip_radial: bfloat16 [128, 64], P(None, 'chan'), may hold values from -0.5 to 0.5
- triplet_bilinear_weight: bfloat16 [16, 64, 64], P(None, 'chan'), may hold values from -0.1875 to 0.1875
- trip_up: bfloat16 [64, 512], P(None, 'chan'), may hold values from -0.75 to 0.75
- quad_down: bfloat16 [512, 32], P(None, 'chan'), may hold values from -0.25 to 0.25
- quad_radial: bfloat16 [128, 32], P(None, 'chan'), may hold values from -0.5 to 0.5
- quad_bilinear: bfloat16 [32, 32, 32], P(None, 'chan'), may hold values from -0.1875 to 0.1875
- quad_up: bfloat16 [32, 512], P(None, 'chan'), may hold values from -1 to 1
- source_proj: bfloat16 [256, 512], P(None, 'chan'), may hold values from -0.375 to 0.375
- target_proj: bfloat16 [256, 512], P(None, 'chan'), may hold values from -0.375 to 0.375
- resid_first: bfloat16 [512, 512], P(None, 'chan'), may hold values from -0.25 to 0.25
- resid_second: bfloat16 [512, 512], P('chan'), may hold values from -0.25 to 0.25
- edge_to_atom: bfloat16 [512, 256], P('chan'), may hold values from -0.046875 to 0.046875
- atom_update: bfloat16 [256, 256], replicated, may hold values from -0.375 to 0.375
- output_first: bfloat16 [256, 256], replicated, may hold values from -0.375 to 0.375
- output_second: bfloat16 [256], replicated, may hold values from -0.375 to 0.375
- tag_table: bfloat16 [3, 256], replicated, may hold values from -3 to 3
- grad_edges: bfloat16 [32768, 512], P('edge', 'chan'), may hold values from -6 to 6
- grad_atoms: bfloat16 [1024, 256], P('edge'), may hold values from -6 to 6
- grad_energy: float32 [1024], P('edge'), may hold values from -6 to 6
Outputs:
- edges_out: bfloat16 [32768, 512], P('edge', 'chan')
- atoms_out: bfloat16 [1024, 256], P('edge')
- energy: float32 [1024], P('edge')
- edge_grad: float32 [32768, 512], P('edge', 'chan')
- atom_grad: float32 [1024, 256], P('edge')
- trip_down_grad: float32 [512, 64], P(None, 'chan')
- trip_radial_grad: float32 [128, 64], P(None, 'chan')
- trip_bilinear_grad: float32 [16, 64, 64], P(None, 'chan')
- trip_up_grad: float32 [64, 512], P(None, 'chan')
- quad_down_grad: float32 [512, 32], P(None, 'chan')
- quad_radial_grad: float32 [128, 32], P(None, 'chan')
- quad_bilinear_grad: float32 [32, 32, 32], P(None, 'chan')
- quad_up_grad: float32 [32, 512], P(None, 'chan')
- source_proj_grad: float32 [256, 512], P(None, 'chan')
- target_proj_grad: float32 [256, 512], P(None, 'chan')
- resid_first_grad: float32 [512, 512], P(None, 'chan')
- resid_second_grad: float32 [512, 512], P('chan')
- edge_to_atom_grad: float32 [512, 256], P('chan')
- atom_update_grad: float32 [256, 256], replicated
- output_first_grad: float32 [256, 256], replicated
- output_second_grad: float32 [256], replicated
- tag_table_grad: float32 [3, 256], replicated
Inputs may be any that keep to these rules, and one draw needn't show every extreme that they name: `edge_source`: partition q holds edges q * 4096 to (q + 1) * 4096 - 1 and atoms q * 128 to (q + 1) * 128 - 1. The source atom of an edge lies in the edge's partition or in the partition just before or after it, the partitions closing into a loop. `edge_target`: the target atom of an edge lies in the edge's own partition. `trip_source`: values below 4096 name an edge of the partition before the slot's edge, the next 4096 one of its own partition, the last 4096 one of the partition after it, the partitions closing into a loop. `quad_source`: values below 4096 name an edge of the partition before the slot's edge, the next 4096 one of its own partition, the last 4096 one of the partition after it, the partitions closing into a loop.
All inputs are finite; a program needn't handle non-finite values.
Results may differ from a plain program's by a relative error of at most 0.014.
Values may be sent and summed in bfloat16 or wider, within the bound.
No kernel may reach another device: no remote copies, remote signals or barrier semaphores. Data moves between devices by JAX's collectives and lax.ppermute only.
A program may use at most 320 MiB of HBM per device.

v0:
```python
import functools

import jax
import jax.numpy as jnp
from jax import lax
from jax.experimental import pallas as pl
from jax.experimental.pallas import tpu as pltpu
from jax.sharding import PartitionSpec as P

TAGS = 3
LANES = 128
BLOCK = 16
BF16 = jnp.bfloat16
F32 = jnp.float32
HIGHEST = lax.Precision.HIGHEST


def chan_swap(value, mask):
    count = lax.axis_size("chan")
    return lax.ppermute(value, "chan", [(i, i ^ mask) for i in range(count)])


def edge_swap(value, mask):
    count = lax.axis_size("edge")
    return lax.ppermute(value, "edge", [(i, i ^ mask) for i in range(count)])


def edge_shift(value, step):
    count = lax.axis_size("edge")
    return lax.ppermute(value, "edge", [(i, (i + step) % count) for i in range(count)])


def gate(*values):
    return list(lax.optimization_barrier(values))


def gather_direct(value):
    return [value] + [chan_swap(value, step) for step in (1, 2, 3)]


def pick(blocks, place):
    return lax.dynamic_index_in_dim(blocks, place, 0, keepdims=False)


def reorder(blocks, rank):
    low_bit = (rank & 1) == 1
    high_bit = (rank & 2) == 2
    first = [jnp.where(low_bit, blocks[i ^ 1], blocks[i]) for i in range(4)]
    return [jnp.where(high_bit, first[i ^ 2], first[i]) for i in range(4)]


def gather_chan(value):
    across = chan_swap(value, 2)
    beside = chan_swap(jnp.stack([value, across]), 1)
    return [value, beside[0], across, beside[1]]


def exchange(blocks, rank):
    got = [pick(blocks, rank)]
    for step in (1, 2, 3):
        got.append(chan_swap(pick(blocks, rank ^ step), step))
    return reorder(got, rank)


def silu_grad(pre_act):
    sigmoid = jax.nn.sigmoid(pre_act)
    return sigmoid * (1.0 + pre_act * (1.0 - sigmoid))


def matmul(first_op, second_op):
    return jnp.dot(first_op, second_op, preferred_element_type=F32)


def inner(first_op, second_op):
    return lax.dot_general(
        first_op, second_op, (((0,), (0,)), ((), ())), preferred_element_type=F32
    )


def outer(first_op, second_op):
    return lax.dot_general(
        first_op, second_op, (((1,), (1,)), ((), ())), preferred_element_type=F32
    )


def block_weights(basis_ref, block, diagonal):
    basis = basis_ref[block].astype(F32)
    count, width = basis.shape
    spread = jnp.broadcast_to(basis[:, None, :], (count, BLOCK, width))
    spread = spread.reshape(count * BLOCK, width)
    return jnp.where(diagonal, spread, 0.0).astype(BF16)


def diagonal_mask(rows, width):
    row = lax.broadcasted_iota(jnp.int32, (rows, width), 0) % BLOCK
    col = lax.broadcasted_iota(jnp.int32, (rows, width), 1) % BLOCK
    return row == col


def lane_groups(value, width):
    group = lax.broadcasted_iota(jnp.int32, value.shape, 1) // width
    zero = jnp.zeros_like(value)
    masked = [jnp.where(group == fold, value, zero) for fold in range(LANES // width)]
    return jnp.concatenate(masked, axis=0)


def slot_copies(whole_ref, slot_refs, sems, first):
    copies = []
    for slot, slot_ref in enumerate(slot_refs):
        size = slot_ref.shape[0]
        copies.append(
            pltpu.make_async_copy(
                whole_ref.at[pl.ds(slot * size, size)], slot_ref, sems.at[first + slot]
            )
        )
    return copies


def gather_body(index_ref, basis_ref, bilinear_ref, *refs, folds, first_row, count):
    packed_refs = refs[:count]
    slots = basis_ref.shape[2] // BLOCK
    agg_ref, sum_ref, table, rows_a, rows_b, sems = refs[-6 - slots : -slots]
    slot_refs = refs[-slots:]
    copies = slot_copies(index_ref, slot_refs, sems, 0)
    for copy in copies:
        copy.start()
    groups, edges, _ = sum_ref.shape
    basis_count = groups * folds
    width = LANES // folds
    piece_rows = edges // folds
    step = min(piece_rows, 64 // folds)
    lane = lax.broadcasted_iota(jnp.int32, (step, LANES), 1) // width

    def unpack(turn, _):
        start = pl.multiple_of(turn * step, step)
        for piece, packed_ref in enumerate(packed_refs):
            values = packed_ref[pl.ds(first_row + start, step), :].astype(F32)
            turned = [values] + [
                pltpu.roll(values, shift * width, 1) for shift in range(1, folds)
            ]
            for fold in range(folds):
                place = pl.multiple_of((piece * folds + fold) * piece_rows + start, step)
                spread = turned[(0 - fold) % folds]
                for group in range(1, folds):
                    spread = jnp.where(lane == group, turned[(group - fold) % folds], spread)
                table[pl.ds(place, step), :] = spread
        return 0

    lax.fori_loop(0, piece_rows // step, unpack, 0)
    for copy in copies:
        copy.wait()
    diagonal = diagonal_mask(basis_count * BLOCK, slots * BLOCK)

    def fetch(block, rows):
        base = block * BLOCK
        for within in range(BLOCK):
            edge = base + within
            for slot in range(slots):
                place = slot_refs[slot][edge]
                at = slot * BLOCK + within
                rows[pl.ds(at, 1), :] = table[pl.ds(place, 1), :]

    def combine(block, values):
        weights = block_weights(basis_ref, block, diagonal)
        each = groups * BLOCK
        joined = jnp.concatenate(
            [weights[fold * each : (fold + 1) * each] for fold in range(folds)], axis=1
        )
        got = matmul(joined, lane_groups(values, width)).astype(BF16)
        start = pl.multiple_of(block * BLOCK, BLOCK)
        sum_ref[:, pl.ds(start, BLOCK), :] = got.reshape(groups, BLOCK, LANES)

    blocks = edges // BLOCK
    fetch(0, rows_a)
    fetch(1, rows_b)

    def turn(pair, _):
        values_a = rows_a[...].astype(BF16)
        values_b = rows_b[...].astype(BF16)
        fetch(jnp.minimum(2 * pair + 2, blocks - 1), rows_a)
        fetch(jnp.minimum(2 * pair + 3, blocks - 1), rows_b)
        combine(2 * pair, values_a)
        combine(2 * pair + 1, values_b)
        return 0

    lax.fori_loop(0, blocks // 2, turn, 0)
    total = matmul(sum_ref[0], bilinear_ref[0])
    for group in range(1, groups):
        total = total + matmul(sum_ref[group], bilinear_ref[group])
    agg_ref[...] = total.astype(BF16)


def branch_forward(index, packed, first_row, basis, bilinear, needed, name):
    groups, _, out_width = bilinear.shape
    edges = basis.shape[0] * BLOCK
    folds = basis.shape[1] // groups
    slots = basis.shape[2] // BLOCK
    vmem = pl.BlockSpec(memory_space=pltpu.VMEM)
    return pl.pallas_call(
        functools.partial(
            gather_body, folds=folds, first_row=first_row, count=len(packed)
        ),
        out_shape=(
            jax.ShapeDtypeStruct((edges, out_width), BF16),
            jax.ShapeDtypeStruct((groups, edges, LANES), BF16),
        ),
        in_specs=[pl.BlockSpec(memory_space=pl.ANY)]
        + [vmem] * (2 + len(packed))
        + [pl.BlockSpec(memory_space=pl.ANY)] * len(needed),
        out_specs=(vmem, vmem),
        scratch_shapes=[
            pltpu.VMEM((len(packed) * edges, LANES), F32),
            pltpu.VMEM((basis.shape[2], LANES), F32),
            pltpu.VMEM((basis.shape[2], LANES), F32),
            pltpu.SemaphoreType.DMA((slots,)),
        ]
        + [pltpu.SMEM((edges,), jnp.int32)] * slots,
        compiler_params=pltpu.CompilerParams(vmem_limit_bytes=56 << 20),
        cost_estimate=pl.CostEstimate(flops=20 * 10**9, transcendentals=0, bytes_accessed=10**7),
        name=name,
    )(index, basis, bilinear, *packed, *needed)


def basis_body(rank_ref, trip_vals, trip_keep, quad_vals, quad_keep, trip_ref, quad_ref, trip_rows, quad_rows):
    del rank_ref
    tile_slots = LANES // BLOCK

    def build(vals_ref, keep_ref, out_ref, rows):
        count, slots, _ = vals_ref.shape
        vals = vals_ref[...].astype(F32) * keep_ref[...].astype(F32)[None]
        rows[...] = vals.reshape(count * slots, LANES)
        group = lax.broadcasted_iota(jnp.int32, (count, LANES), 1) // BLOCK
        for tile in range(slots // tile_slots):
            by_slot = [
                rows[pl.ds(tile * tile_slots + slot, count, stride=slots), :]
                for slot in range(tile_slots)
            ]
            for block in range(tile_slots):
                joined = None
                for slot, value in enumerate(by_slot):
                    shift = (slot - block) * BLOCK % LANES
                    turned = pltpu.roll(value, shift, 1) if shift else value
                    joined = turned if joined is None else jnp.where(group == slot, turned, joined)
                out_ref[block, :, tile * LANES : (tile + 1) * LANES] = joined.astype(BF16)

    build(trip_vals, trip_keep, trip_ref, trip_rows)
    build(quad_vals, quad_keep, quad_ref, quad_rows)


def slot_basis(rank, circular, trip_mask, spherical, quad_mask, edges):
    steps = edges // LANES
    blocks = LANES // BLOCK

    def source(array):
        shape = array.shape[:-1] + (LANES,)
        lead = (0,) * (len(shape) - 1)
        return pl.BlockSpec(shape, lambda step, rank_ref: lead + (rank_ref[0] * steps + step,))

    def target(count, slots):
        return pl.BlockSpec((blocks, count, slots * BLOCK), lambda step, rank_ref: (step, 0, 0))

    def shape_of(array):
        count, slots, _ = array.shape
        return jax.ShapeDtypeStruct((edges // BLOCK, count, slots * BLOCK), BF16)

    def rows_of(array):
        return pltpu.VMEM((array.shape[0] * array.shape[1], LANES), F32)

    return pl.pallas_call(
        basis_body,
        grid_spec=pltpu.PrefetchScalarGridSpec(
            num_scalar_prefetch=1,
            grid=(steps,),
            in_specs=[source(circular), source(trip_mask), source(spherical), source(quad_mask)],
            out_specs=[target(*circular.shape[:2]), target(*spherical.shape[:2])],
            scratch_shapes=[rows_of(circular), rows_of(spherical)],
        ),
        out_shape=(shape_of(circular), shape_of(spherical)),
        cost_estimate=pl.CostEstimate(flops=10 * 10**9, transcendentals=0, bytes_accessed=10**7),
        name="slot_basis",
    )(rank[None], circular, trip_mask, spherical, quad_mask)


TABLES = 4


def scatter_body(
    index_ref, same_ref, basis_ref, grad_ref, bilinear_ref, *refs, folds, owners, needed
):
    refs = refs[needed:]
    packed_refs = refs[:owners]
    slots = basis_ref.shape[2] // BLOCK
    part, rows_a, rows_b = refs[owners : owners + 3]
    tables = refs[owners + 3 : owners + 3 + TABLES]
    sems = refs[owners + 3 + TABLES]
    slot_refs = refs[-2 * slots : -slots]
    same_refs = refs[-slots:]
    copies = slot_copies(index_ref, slot_refs, sems, 0)
    copies += slot_copies(same_ref, same_refs, sems, slots)
    for copy in copies:
        copy.start()
    sides, piece_rows, _ = packed_refs[0].shape
    groups, edges, _ = part.shape
    basis_count = groups * folds
    width = LANES // folds
    chunk = 256
    table_rows = tables[0].shape[0]

    def clear(turn, _):
        start = pl.multiple_of(turn * chunk, chunk)
        for table in tables:
            table[pl.ds(start, chunk), :] = jnp.zeros((chunk, LANES), F32)
        return 0

    lax.fori_loop(0, table_rows // chunk, clear, 0)
    for group in range(groups):
        part[group] = outer(grad_ref[...], bilinear_ref[group]).astype(BF16)
    for copy in copies:
        copy.wait()
    diagonal = diagonal_mask(basis_count * BLOCK, slots * BLOCK)

    def spread(block, rows):
        weights = block_weights(basis_ref, block, diagonal)
        start = pl.multiple_of(block * BLOCK, BLOCK)
        values = part[:, pl.ds(start, BLOCK), :].reshape(groups * BLOCK, LANES)
        rows[...] = inner(weights, lane_groups(values, width))

    def store(block, rows):
        base = block * BLOCK
        for within in range(0, BLOCK, 2):
            edge = base + within
            next_edge = edge + 1
            for slot in range(slots):
                table = tables[slot % TABLES]
                at = slot * BLOCK + within
                place = slot_refs[slot][edge]
                next_place = slot_refs[slot][next_edge]
                same = same_refs[slot][edge]
                value = rows[pl.ds(at, 1), :]
                next_value = rows[pl.ds(at + 1, 1), :] + same * value
                total = table[pl.ds(place, 1), :] + value
                next_total = table[pl.ds(next_place, 1), :] + next_value
                table[pl.ds(place, 1), :] = total
                table[pl.ds(next_place, 1), :] = next_total

    blocks = edges // BLOCK
    spread(0, rows_a)

    def turn(pair, _):
        spread(2 * pair + 1, rows_b)
        store(2 * pair, rows_a)
        spread(jnp.minimum(2 * pair + 2, blocks - 1), rows_a)
        store(2 * pair + 1, rows_b)
        return 0

    lax.fori_loop(0, blocks // 2, turn, 0)
    step = min(piece_rows, 64 // folds)
    per_piece = piece_rows // step
    lane = lax.broadcasted_iota(jnp.int32, (step, LANES), 1) // width
    low = lane < folds // 2
    even = lane % 2 == 0

    def join(first, second):
        return jnp.where(low, first, second) + pltpu.roll(
            jnp.where(low, second, first), LANES // 2, 1
        )

    def pack(turn, _):
        side = turn // per_piece
        start = pl.multiple_of((turn % per_piece) * step, step)
        for owner, packed_ref in enumerate(packed_refs):
            piece = side * owners + owner
            sums = []
            for fold in range(folds):
                place = pl.multiple_of((piece * folds + fold) * piece_rows + start, step)
                total = tables[0][pl.ds(place, step), :]
                for table in tables[1:]:
                    total = total + table[pl.ds(place, step), :]
                sums.append(total)
            if folds == 2:
                joined = join(sums[0], sums[1])
            else:
                first, second = join(sums[0], sums[2]), join(sums[1], sums[3])
                joined = jnp.where(
                    even,
                    first + pltpu.roll(first, LANES - width, 1),
                    second + pltpu.roll(second, width, 1),
                )
            packed_ref[side, pl.ds(start, step), :] = joined.astype(BF16)
        return 0

    lax.fori_loop(0, sides * per_piece, pack, 0)


def branch_backward(index, basis, grad, bilinear, sides, owners, needed, name):
    edges = grad.shape[0]
    groups = bilinear.shape[0]
    folds = basis.shape[1] // groups
    vmem = pl.BlockSpec(memory_space=pltpu.VMEM)
    out = jax.ShapeDtypeStruct((sides, edges // folds, LANES), BF16)
    slots = basis.shape[2] // BLOCK
    same = (index == jnp.roll(index, -1)).astype(F32)
    whole = pl.BlockSpec(memory_space=pl.ANY)
    return pl.pallas_call(
        functools.partial(scatter_body, folds=folds, owners=owners, needed=len(needed)),
        out_shape=(out,) * owners,
        in_specs=[whole, whole, vmem, vmem, vmem]
        + [pl.BlockSpec(memory_space=pl.ANY)] * len(needed),
        out_specs=(vmem,) * owners,
        scratch_shapes=[
            pltpu.VMEM((groups, edges, LANES), BF16),
            pltpu.VMEM((basis.shape[2], LANES), F32),
            pltpu.VMEM((basis.shape[2], LANES), F32),
        ]
        + [pltpu.VMEM((sides * owners * edges, LANES), F32)] * TABLES
        + [pltpu.SemaphoreType.DMA((2 * slots,))]
        + [pltpu.SMEM((edges,), jnp.int32)] * slots
        + [pltpu.SMEM((edges,), F32)] * slots,
        compiler_params=pltpu.CompilerParams(vmem_limit_bytes=58 << 20),
        cost_estimate=pl.CostEstimate(flops=20 * 10**9, transcendentals=0, bytes_accessed=10**7),
        name=name,
    )(index, same, basis, grad, bilinear, *needed)


def large_parts(refs, block_ref, first, place):
    trip_up, quad_up, proj, first_layer, second_layer, to_atom = refs
    lanes = pl.ds(pl.multiple_of(place * LANES, LANES), LANES)
    for whole in (trip_up, quad_up, proj, first_layer):
        count = whole.shape[0]
        yield block_ref.at[pl.ds(first, count)], whole.at[:, lanes]
        first += count
    for whole in (second_layer, to_atom):
        for column in range(0, whole.shape[1], LANES):
            yield block_ref.at[pl.ds(first, LANES)], whole.at[lanes, pl.ds(column, LANES)]
            first += LANES


def unpack_body(rank_ref, *refs, owners):
    for owner in range(owners):
        for block, window in large_parts(refs[owners:], refs[owner], 0, rank_ref[0] ^ owner):
            window[...] = block[...]


def unpack_large(rank, blocks, shapes):
    vmem = pl.BlockSpec(memory_space=pltpu.VMEM)
    return pl.pallas_call(
        functools.partial(unpack_body, owners=len(blocks)),
        out_shape=tuple(jax.ShapeDtypeStruct(shape, BF16) for shape in shapes),
        in_specs=[pl.BlockSpec(memory_space=pltpu.SMEM)] + [vmem] * len(blocks),
        out_specs=(vmem,) * len(shapes),
        compiler_params=pltpu.CompilerParams(vmem_limit_bytes=32 << 20),
        name="unpack_large",
    )(rank[None], *blocks)


def pack_body(rank_ref, *refs, owners, count):
    large, trip_bil, quad_bil, atoms = refs[:6], refs[6], refs[7], refs[8]
    for owner, out_ref in enumerate(refs[count : count + owners]):
        place = rank_ref[0] ^ owner
        row = 0
        for block, window in large_parts(large, out_ref, 0, place):
            block[...] = window[...]
            row += block.shape[0]
        for whole in (trip_bil, quad_bil):
            groups, rows, out = whole.shape
            folds = LANES // out
            each = rows // folds // owners
            together = 16 // each
            for group in range(0, groups, together):
                pieces = [
                    jnp.concatenate(
                        [
                            whole[
                                member,
                                pl.ds(pl.multiple_of(fold * rows // folds + place * each, each), each),
                                :,
                            ]
                            for fold in range(folds)
                        ],
                        axis=1,
                    )
                    for member in range(group, group + together)
                ]
                out_ref[row : row + 16, :] = jnp.concatenate(pieces, axis=0).astype(BF16)
                row += 16
        for column in range(0, atoms.shape[1], LANES):
            out_ref[row : row + atoms.shape[0], :] = atoms[:, column : column + LANES]
            row += atoms.shape[0]


def pack_early(rank, members, owners, needed):
    total = sum(member.size for member in members[:-1]) // owners // LANES
    total += members[-1].size // LANES
    out = jax.ShapeDtypeStruct((total, LANES), BF16)
    vmem = pl.BlockSpec(memory_space=pltpu.VMEM)
    return pl.pallas_call(
        functools.partial(pack_body, owners=owners, count=len(members) + len(needed)),
        out_shape=(out,) * owners,
        in_specs=[pl.BlockSpec(memory_space=pltpu.SMEM)]
        + [vmem] * len(members)
        + [pl.BlockSpec(memory_space=pl.ANY)] * len(needed),
        out_specs=(vmem,) * owners,
        compiler_params=pltpu.CompilerParams(vmem_limit_bytes=32 << 20),
        cost_estimate=pl.CostEstimate(flops=20 * 10**9, transcendentals=0, bytes_accessed=10**7),
        name="pack_early",
    )(rank[None], *members, *needed)


def fold_lanes(rows):
    count, width = rows.shape
    folds = LANES // width
    each = count // folds
    return jnp.concatenate([rows[i * each : (i + 1) * each] for i in range(folds)], axis=1)


def unfold_lanes(packed, width):
    folds = LANES // width
    return jnp.concatenate([packed[:, i * width : (i + 1) * width] for i in range(folds)], axis=0)


def columns(array):
    return jnp.concatenate(
        [array[:, i : i + LANES] for i in range(0, array.shape[1], LANES)], axis=0
    )


def uncolumns(rows, width):
    each = rows.shape[0] * LANES // width
    return jnp.concatenate(
        [rows[i * each : (i + 1) * each] for i in range(width // LANES)], axis=1
    )


def edge_steps():
    steps = []
    size = 1
    while size < lax.axis_size("edge"):
        steps.append(size)
        size *= 2
    return steps


def halve(value, mask):
    bit = (lax.axis_index("edge") & mask) != 0
    half = value.shape[0] // 2
    keep = jnp.where(bit, value[half:], value[:half])
    send = jnp.where(bit, value[:half], value[half:])
    return keep, send


def join_halves(value, mask):
    bit = (lax.axis_index("edge") & mask) != 0
    got = edge_swap(value, mask)
    return jnp.concatenate([jnp.where(bit, got, value), jnp.where(bit, value, got)], axis=0)


def tree_sum(values):
    values = [value.astype(F32) for value in values]
    while len(values) > 1:
        values = [values[i] + values[i + 1] for i in range(0, len(values), 2)]
    return values[0]


def edge_total(value):
    for mask in edge_steps():
        value = (value.astype(F32) + edge_swap(value, mask).astype(F32)).astype(BF16)
    return value


def per_device(
    edge_emb,
    atom_emb,
    radial,
    circular,
    spherical,
    atom_tags,
    edge_source,
    edge_target,
    trip_source,
    trip_mask,
    quad_source,
    quad_mask,
    triplet_down_weight,
    trip_radial,
    triplet_bilinear_weight,
    trip_up,
    quad_down,
    quad_radial,
    quad_bilinear,
    quad_up,
    source_proj,
    target_proj,
    resid_first,
    resid_second,
    edge_to_atom,
    atom_update,
    output_first,
    output_second,
    tag_table,
    grad_edges,
    grad_atoms,
    grad_energy,
):
    edges_here = edge_emb.shape[0]
    atoms_here = atom_emb.shape[0]
    parts = lax.axis_size("chan")
    edge_parts = lax.axis_size("edge")
    rank = lax.axis_index("chan")
    edge_rank = lax.axis_index("edge")
    edges = edges_here // parts
    cols = edge_emb.shape[1]
    start = rank * edges

    def own(array, axis):
        return lax.dynamic_slice_in_dim(array, start, edges, axis)

    edge_blocks = edge_emb.reshape(parts, edges, cols)
    edge_sent = [pick(edge_blocks, rank ^ step) for step in range(parts)]
    *edge_sent, triplet_down_weight, trip_radial, triplet_bilinear_weight, quad_bilinear = gate(
        *edge_sent, triplet_down_weight, trip_radial, triplet_bilinear_weight, quad_bilinear
    )
    edge_got = [edge_sent[0]] + [chan_swap(edge_sent[step], step) for step in range(1, parts)]
    own_edges = jnp.concatenate(reorder(edge_got, rank), axis=1)

    trip_cols = triplet_down_weight.shape[1]
    quad_cols = quad_down.shape[1]
    trip_out = triplet_bilinear_weight.shape[2]
    quad_out = quad_bilinear.shape[2]
    down_own = jnp.concatenate([triplet_down_weight, quad_down], axis=1)
    small = jnp.concatenate(
        [
            columns(
                jnp.concatenate(
                    [down_own, jnp.concatenate([trip_radial, quad_radial], axis=1)], axis=0
                ).T
            ),
            fold_lanes(triplet_bilinear_weight.reshape(-1, trip_out)),
            fold_lanes(quad_bilinear.reshape(-1, quad_out)),
        ],
        axis=0,
    )
    small = reorder(gather_direct(small), rank)
    channels = parts * cols
    long = channels + radial.shape[1]
    small_rows = (trip_cols + quad_cols) * long // LANES
    trip_bil_rows = triplet_bilinear_weight.size // LANES
    downs = jnp.stack([uncolumns(block[:small_rows], long) for block in small])
    trip_both = downs[:, :trip_cols].reshape(parts * trip_cols, -1).T
    quad_both = downs[:, trip_cols:].reshape(parts * quad_cols, -1).T
    both = jnp.concatenate([trip_both, quad_both], axis=1)
    down_full, radial_full = both[:channels], both[channels:]
    trip_width = trip_both.shape[1]
    quad_width = quad_both.shape[1]
    trip_folds = LANES // trip_width
    quad_folds = LANES // quad_width

    def group_rows(blocks, shape, folds):
        whole = jnp.concatenate(
            [unfold_lanes(block, shape[2]).reshape(shape) for block in blocks], axis=1
        )
        count, width, out = whole.shape
        split = whole.reshape(folds, count // folds, width, out)
        return jnp.transpose(split, (1, 0, 2, 3)).reshape(count // folds, folds * width, out)

    trip_bil = group_rows(
        [block[small_rows : small_rows + trip_bil_rows] for block in small],
        triplet_bilinear_weight.shape,
        trip_folds,
    )
    quad_bil = group_rows(
        [block[small_rows + trip_bil_rows :] for block in small],
        quad_bilinear.shape,
        quad_folds,
    )

    own_radial = own(radial, 0)
    down_pre = matmul(own_edges, down_full)
    radial_pre = matmul(own_radial, radial_full)
    dense = (jax.nn.silu(down_pre) * radial_pre).astype(BF16)
    trip_piece = fold_lanes(dense[:, :trip_width])
    quad_piece = fold_lanes(dense[:, trip_width:])
    trip_rows = trip_piece.shape[0]
    wire = jnp.concatenate([trip_piece, quad_piece], axis=0)
    rank_now, wire, *members, atom_emb, grad_edges = gate(
        rank,
        wire,
        trip_up,
        quad_up,
        source_proj,
        target_proj,
        resid_first,
        resid_second,
        edge_to_atom,
        atom_emb,
        grad_edges,
    )
    before = edge_shift(wire, 1)
    later = edge_shift(wire, -1)
    own_across = chan_swap(wire, 2)
    own_beside = chan_swap(wire, 1)

    def spread(first, across):
        return [first, chan_swap(first, 1), across, chan_swap(across, 1)]

    before_across = chan_swap(before, 2)
    later_across = chan_swap(later, 2)
    wire_pieces = (
        spread(before, before_across)
        + [wire, own_beside, own_across, chan_swap(own_across, 1)]
        + spread(later, later_across)
    )

    def places(source):
        local = own(source, 1)
        within = local % edges_here
        owner = (within // edges) ^ rank
        return ((local // edges_here) * edges_here + owner * edges + within % edges).reshape(-1)

    trip_index = places(trip_source)
    quad_index = places(quad_source)
    trip_basis, quad_basis = slot_basis(
        rank_now, circular, trip_mask, spherical, quad_mask, edges
    )

    large = jnp.concatenate(members[:5] + [columns(members[5]), columns(members[6])], axis=0)
    tag_onehot = (atom_tags[:, None] == jnp.arange(TAGS)[None, :]).astype(F32)
    atom_full = atom_emb.astype(F32) + jnp.dot(
        tag_onehot, tag_table.astype(F32), precision=HIGHEST
    )
    atom_low = atom_full.astype(BF16)
    grad_blocks = grad_edges.reshape(parts, edges, cols)
    grad_sent = [pick(grad_blocks, rank ^ step) for step in range(parts)]
    quad_agg, quad_sum = branch_forward(
        quad_index,
        wire_pieces,
        trip_rows,
        quad_basis,
        quad_bil,
        [large, atom_low] + grad_sent,
        "quad_gather",
    )
    large_across, large_beside, atom_before, atom_later, quad_agg, *grad_sent = gate(
        chan_swap(large, 2),
        chan_swap(large, 1),
        edge_shift(atom_low, 1),
        edge_shift(atom_low, -1),
        quad_agg,
        *grad_sent,
    )

    trip_agg, trip_sum = branch_forward(
        trip_index,
        wire_pieces,
        0,
        trip_basis,
        trip_bil,
        [large_across, atom_before, atom_later] + grad_sent,
        "trip_gather",
    )
    grad_got = [grad_sent[0]] + [chan_swap(grad_sent[step], step) for step in range(1, parts)]
    large_diag, trip_agg, *grad_got = gate(chan_swap(large_across, 1), trip_agg, *grad_got)
    grad_two = jnp.concatenate(reorder(grad_got, rank), axis=1)
    sizes = [
        trip_up.shape[0],
        quad_up.shape[0],
        source_proj.shape[0],
        target_proj.shape[0],
        resid_first.shape[0],
        resid_second.size // LANES,
        edge_to_atom.size // LANES,
    ]

    def offsets_of(sizes):
        return [sum(sizes[:i]) for i in range(len(sizes) + 1)]

    offsets = offsets_of(sizes)

    trip_up_full, quad_up_full, proj_full, first_full, second_full, to_atom_full = unpack_large(
        rank,
        [large, large_beside, large_across, large_diag],
        [
            (trip_width, channels),
            (quad_width, channels),
            (2 * source_proj.shape[0], channels),
            (channels, channels),
            (channels, channels),
            (channels, edge_to_atom.shape[1]),
        ],
    )

    atom_wide = jnp.concatenate([atom_before, atom_low, atom_later], axis=0)
    atom_total = edge_parts * atoms_here
    source_local = (own(edge_source, 0) - (edge_rank - 1) * atoms_here) % atom_total
    target_local = own(edge_target, 0) - edge_rank * atoms_here
    source_hot = (source_local[:, None] == jnp.arange(3 * atoms_here)[None, :]).astype(BF16)
    target_hot = (target_local[:, None] == jnp.arange(atoms_here)[None, :]).astype(BF16)
    ends = jnp.concatenate(
        [
            matmul(source_hot, atom_wide).astype(BF16),
            matmul(target_hot, atom_low).astype(BF16),
        ],
        axis=1,
    )

    message = matmul(ends, proj_full)
    trip_out_pre = matmul(trip_agg, trip_up_full)
    quad_out_pre = matmul(quad_agg, quad_up_full)
    hidden_one = (
        own_edges.astype(F32)
        + jax.nn.silu(trip_out_pre)
        + jax.nn.silu(quad_out_pre)
        + jax.nn.silu(message)
    )
    hidden_low = hidden_one.astype(BF16)
    first_pre = matmul(hidden_low, first_full)
    first_low = jax.nn.silu(first_pre).astype(BF16)
    second_pre = matmul(first_low, second_full)
    edges_low = (hidden_one + jax.nn.silu(second_pre)).astype(BF16)
    edge_sums = inner(target_hot, edges_low)
    sums_high = edge_sums.astype(BF16)
    sums_rest = (edge_sums - sums_high.astype(F32)).astype(BF16)
    atom_sum = matmul(sums_high, to_atom_full) + matmul(sums_rest, to_atom_full)
    atom_sum = atom_sum + chan_swap(atom_sum, 1)
    atom_sum = atom_sum + chan_swap(atom_sum, 2)
    atom_sum, edges_low = gate(atom_sum, edges_low)

    atom_sum_low = atom_sum.astype(BF16)
    update_pre = matmul(atom_sum_low, atom_update)
    atoms_new = atom_full + jax.nn.silu(update_pre)
    atoms_low = atoms_new.astype(BF16)
    output_pre = matmul(atoms_low, output_first)
    output_low = jax.nn.silu(output_pre).astype(BF16)
    energy = matmul(output_low, output_second)
    output_second_grad = jnp.dot(grad_energy, output_low.astype(F32), precision=HIGHEST)
    output_grad = (
        grad_energy[:, None] * output_second.astype(F32)[None, :] * silu_grad(output_pre)
    ).astype(BF16)
    output_first_grad = inner(atoms_low, output_grad)
    atoms_new_grad = grad_atoms.astype(F32) + outer(output_grad, output_first)
    update_grad = (atoms_new_grad * silu_grad(update_pre)).astype(BF16)
    atom_update_grad = inner(atom_sum_low, update_grad)
    atom_sum_grad = outer(update_grad, atom_update).astype(BF16)

    edge_part_grad = matmul(target_hot, atom_sum_grad).astype(BF16)
    edge_to_atom_grad = inner(edges_low, edge_part_grad)
    two_grad = grad_two.astype(F32) + outer(edge_part_grad, to_atom_full)
    second_grad = (two_grad * silu_grad(second_pre)).astype(BF16)
    resid_second_grad = inner(first_low, second_grad)
    first_grad = (outer(second_grad, second_full) * silu_grad(first_pre)).astype(BF16)
    resid_first_grad = inner(hidden_low, first_grad)
    one_grad = two_grad + outer(first_grad, first_full)
    trip_out_grad = (one_grad * silu_grad(trip_out_pre)).astype(BF16)
    quad_out_grad = (one_grad * silu_grad(quad_out_pre)).astype(BF16)
    message_grad = (one_grad * silu_grad(message)).astype(BF16)
    trip_up_grad = inner(trip_agg, trip_out_grad)
    quad_up_grad = inner(quad_agg, quad_out_grad)
    trip_agg_grad = outer(trip_out_grad, trip_up_full).astype(BF16)
    quad_agg_grad = outer(quad_out_grad, quad_up_full).astype(BF16)
    proj_grad = inner(ends, message_grad)
    width = atom_low.shape[1]
    source_sums = inner(source_hot, message_grad).astype(BF16)
    target_sums = inner(target_hot, message_grad).astype(BF16)
    source_back = outer(source_sums, proj_full[:width])
    target_back = outer(target_sums, proj_full[width:])
    wide_atoms = source_back.reshape(3, atoms_here, width)
    wide_atoms = wide_atoms.at[1].add(target_back)

    def split(array, axis):
        return jnp.split(array, parts, axis=axis)

    def pack(members):
        packed = [
            jnp.concatenate([member[i] for member in members], axis=0).astype(BF16)
            for i in range(parts)
        ]
        return reorder(packed, rank)

    trip_bilinear_grad = jnp.einsum(
        "gej,eo->gjo", trip_sum, trip_agg_grad, preferred_element_type=F32
    )
    quad_bilinear_grad = jnp.einsum(
        "gej,eo->gjo", quad_sum, quad_agg_grad, preferred_element_type=F32
    )
    atom_rows = jnp.concatenate(
        [columns(atom_update_grad), columns(output_first_grad)], axis=0
    ).astype(BF16)
    atom_quarter = pick(atom_rows.reshape(parts, -1, LANES), rank)

    def send_back(array):
        blocks = jnp.stack([array[:, i * cols : (i + 1) * cols] for i in range(parts)])
        return [pick(blocks, rank ^ step) for step in range(parts)]

    def receive(sent):
        return [sent[0]] + [chan_swap(sent[step], step) for step in range(1, parts)]

    out_sent = send_back(edges_low)
    packed = pack_early(
        rank,
        [
            trip_up_grad.astype(BF16),
            quad_up_grad.astype(BF16),
            proj_grad.astype(BF16),
            resid_first_grad.astype(BF16),
            resid_second_grad.astype(BF16),
            edge_to_atom_grad.astype(BF16),
            trip_bilinear_grad,
            quad_bilinear_grad,
            wide_atoms.reshape(3 * atoms_here, width).astype(BF16),
        ],
        parts,
        out_sent,
    )
    *out_got, own_packed = gate(*receive(out_sent), packed[0])
    packed = [own_packed] + list(packed[1:])
    edges_out = jnp.concatenate(reorder(out_got, rank), axis=0)

    trip_tables = branch_backward(
        trip_index,
        trip_basis,
        trip_agg_grad,
        trip_bil,
        3,
        parts,
        [edges_out] + packed,
        "trip_scatter",
    )
    *packed_got, own_table = gate(*receive(packed), trip_tables[0])
    trip_tables = [own_table] + list(trip_tables[1:])
    mine = tree_sum(packed_got)
    early = packed[0].shape[0] - 3 * atoms_here * width // LANES
    wide_sum = uncolumns(mine[early:], width).reshape(3, atoms_here, width)
    early_rows = jnp.concatenate([mine[:early].astype(BF16), atom_quarter], axis=0)
    total_rows = early_rows.shape[0]
    early_rows = jnp.pad(early_rows, ((0, -total_rows % (16 * edge_parts)), (0, 0)))
    steps = edge_steps()
    keep, send = halve(early_rows, steps[0])

    quad_tables = branch_backward(
        quad_index,
        quad_basis,
        quad_agg_grad,
        quad_bil,
        3,
        parts,
        [wide_sum, send] + trip_tables,
        "quad_scatter",
    )
    quad_tables = list(quad_tables)
    early_got, *trip_got = gate(
        edge_swap(send, steps[0]), *receive(trip_tables), *quad_tables
    )
    trip_got, quad_tables = trip_got[:parts], trip_got[parts:]
    quad_got = receive(quad_tables)
    early_part = (keep.astype(F32) + early_got.astype(F32)).astype(BF16)
    for mask in steps[1:]:
        keep, send = halve(early_part, mask)
        early_part = (keep.astype(F32) + edge_swap(send, mask).astype(F32)).astype(BF16)

    table = jnp.concatenate(
        [
            tree_sum(trip_got),
            tree_sum(quad_got),
            jnp.stack([columns(wide_sum[side]) for side in range(3)]),
        ],
        axis=1,
    )
    branch_grad = (
        table[1]
        + edge_shift(table[0].astype(BF16), -1).astype(F32)
        + edge_shift(table[2].astype(BF16), 1).astype(F32)
    )
    wire_rows = wire.shape[0]
    atom_grad = atoms_new_grad + uncolumns(branch_grad[wire_rows:], width)
    branch_grad = branch_grad[:wire_rows]
    branch_grad = jnp.concatenate(
        [
            unfold_lanes(branch_grad[:trip_rows], trip_width),
            unfold_lanes(branch_grad[trip_rows:], quad_width),
        ],
        axis=1,
    )
    down_grad = (branch_grad * radial_pre * silu_grad(down_pre)).astype(BF16)
    radial_grad = (branch_grad * jax.nn.silu(down_pre)).astype(BF16)
    down_weight_grad = inner(own_edges, down_grad)
    radial_weight_grad = inner(own_radial, radial_grad)
    edge_grad = (one_grad + outer(down_grad, down_full)).astype(BF16)
    edge_grad = jnp.concatenate(reorder(receive(send_back(edge_grad)), rank), axis=0).astype(F32)

    tag_table_grad = jnp.dot(tag_onehot.T, atom_grad, precision=HIGHEST)
    tiny = columns(jnp.concatenate([output_second_grad[None], tag_table_grad], axis=0))

    small_grad = jnp.concatenate([down_weight_grad, radial_weight_grad], axis=0)
    late_sent = pack(
        [
            [
                columns(jnp.concatenate([trip_block, quad_block], axis=1).T)
                for trip_block, quad_block in zip(
                    split(small_grad[:, :trip_width], 1), split(small_grad[:, trip_width:], 1)
                )
            ]
        ]
    )
    late = tree_sum(receive(late_sent))
    late_rows = late.shape[0]
    late = edge_total(jnp.concatenate([late, tiny], axis=0).astype(BF16)).astype(F32)
    tiny = uncolumns(late[late_rows:], width)
    late = late[:late_rows]
    summed = early_part
    for mask in reversed(steps):
        summed = join_halves(summed, mask)
    summed = summed[:total_rows]
    atom_out = jnp.concatenate(reorder(gather_direct(summed[early:]), rank), axis=0).astype(F32)
    summed = summed[:early].astype(F32)
    sizes = sizes + [trip_bil_rows, quad_bilinear.size // LANES]
    offsets = offsets_of(sizes)
    parts_out = [summed[offsets[i] : offsets[i + 1]] for i in range(len(sizes))]
    small_out = uncolumns(late, long).T
    trip_bil_out, quad_bil_out = parts_out[7:]
    half = atom_out.shape[0] // 2
    return (
        edges_out,
        atoms_low,
        energy,
        edge_grad,
        atom_grad,
        small_out[:channels, :trip_cols],
        small_out[channels:, :trip_cols],
        unfold_lanes(trip_bil_out, trip_out).reshape(triplet_bilinear_weight.shape),
        parts_out[0],
        small_out[:channels, trip_cols:],
        small_out[channels:, trip_cols:],
        unfold_lanes(quad_bil_out, quad_out).reshape(quad_bilinear.shape),
        parts_out[1],
        parts_out[2],
        parts_out[3],
        parts_out[4],
        uncolumns(parts_out[5], resid_second.shape[1]),
        uncolumns(parts_out[6], edge_to_atom.shape[1]),
        uncolumns(atom_out[:half], atom_update.shape[1]),
        uncolumns(atom_out[half:], output_first.shape[1]),
        tiny[0],
        tiny[1:],
    )


def solution(mesh):
    return jax.shard_map(
        per_device,
        mesh=mesh,
        in_specs=(
            P("edge", "chan"),
            P("edge", None),
            P("edge", None),
            P(None, None, "edge"),
            P(None, None, "edge"),
            P("edge"),
            P("edge"),
            P("edge"),
            P(None, "edge"),
            P(None, "edge"),
            P(None, "edge"),
            P(None, "edge"),
            P(None, "chan"),
            P(None, "chan"),
            P(None, "chan", None),
            P(None, "chan"),
            P(None, "chan"),
            P(None, "chan"),
            P(None, "chan", None),
            P(None, "chan"),
            P(None, "chan"),
            P(None, "chan"),
            P(None, "chan"),
            P("chan", None),
            P("chan", None),
            P(),
            P(),
            P(),
            P(),
            P("edge", "chan"),
            P("edge", None),
            P("edge"),
        ),
        out_specs=(
            P("edge", "chan"),
            P("edge", None),
            P("edge"),
            P("edge", "chan"),
            P("edge", None),
            P(None, "chan"),
            P(None, "chan"),
            P(None, "chan", None),
            P(None, "chan"),
            P(None, "chan"),
            P(None, "chan"),
            P(None, "chan", None),
            P(None, "chan"),
            P(None, "chan"),
            P(None, "chan"),
            P(None, "chan"),
            P("chan", None),
            P("chan", None),
            P(),
            P(),
            P(),
            P(),
        ),
        check_vma=False,
    )
```

profile of v0, /device:TPU:0, one launch (start us, length us, event | category | flops | bytes accessed | tf_op | source)
XLA Modules:
  0.0 289.3 jit_solution(5127998303527616944)
XLA Ops:
  3.1 2.6 collective-permute-start.4
  15.8 5.8 %collective-permute-done.1 = bf16[1024,128]{1,0:T(8,128)(2,1)S(1)} collective-permute-done((bf16[1024,128]{1,0:T(8,128)(2,1)S(1)}, bf16[1024,128]{1,0:T(8,128)(2,1)S(1)}, u32[]{:S(2)}, u32[]{:S(2)}) %collective-permute-start.1) | collective-permute-done | bytes 262176 | tf_op jit(solution)/shard_map/ppermute | solution.py:20
  25.8 4.8 %collective-permute-start.17 = (bf16[768,128]{1,0:T(8,128)(2,1)S(1)}, bf16[768,128]{1,0:T(8,128)(2,1)S(1)}, u32[]{:S(2)}, u32[]{:S(2)}) collective-permute-start(bf16[768,128]{1,0:T(8,128)(2,1)S(1)} %maximum_maximum_fusion.2.refs_4_), channel_id=1, source_target_pairs={{0,28},{4,0},{8,4},{12,8},{16,12},{20,16},{24,20},{28,24},{1,29},{... | collective-permute-start | bytes 589832 | tf_op jit(solution)/shard_map/ppermute | solution.py:30
  35.5 6.3 %slot_basis.1 = (bf16[64,16,256]{2,1,0:T(8,128)(2,1)}, bf16[64,32,128]{2,1,0:T(8,128)(2,1)}) custom-call(s32[1]{0:T(128)} %bitcast.20.rank_ref, bf16[16,16,4096]{2,1,0:T(8,128)(2,1)} %trip_vals.1, s32[16,4096]{1,0:T(8,128)} %trip_keep.1, bf16[32,8,4096]{2,1,0:T(8,128)(2,1)} %quad_vals.1, s32[8,4096]{1,0:T(8,128)} %quad_keep.1), custom_call_target="tpu_custom_call" | custom-call | flops 10000000000 | bytes 10000000 | tf_op jit(solution)/shard_map/slot_basis/pallas_call | solution.py:269
  44.7 5.0 %collective-permute-done.19.refs_10_ = bf16[768,128]{1,0:T(8,128)(2,1)S(1)} collective-permute-done((bf16[768,128]{1,0:T(8,128)(2,1)S(1)}, bf16[768,128]{1,0:T(8,128)(2,1)S(1)}, u32[]{:S(2)}, u32[]{:S(2)}) %collective-permute-start.19) | collective-permute-done | bytes 196640 | tf_op jit(solution)/shard_map/ppermute | solution.py:20
  49.7 3.7 %collective-permute-done.12.refs_2_ = bf16[768,128]{1,0:T(8,128)(2,1)S(1)} collective-permute-done((bf16[768,128]{1,0:T(8,128)(2,1)S(1)}, bf16[768,128]{1,0:T(8,128)(2,1)S(1)}, u32[]{:S(2)}, u32[]{:S(2)}) %collective-permute-start.12) | collective-permute-done | bytes 196640 | tf_op jit(solution)/shard_map/ppermute | solution.py:20
  53.5 4.5 %collective-permute-start.9 = (bf16[128,256]{1,0:T(8,128)(2,1)S(1)}, bf16[128,256]{1,0:T(8,128)(2,1)S(1)}, u32[]{:S(2)}, u32[]{:S(2)}) collective-permute-start(bf16[128,256]{1,0:T(8,128)(2,1)S(1)} %get-tuple-element.364.refs_13_), channel_id=1, source_target_pairs={{0,28},{4,0},{8,4},{12,8},{16,12},{20,16},{24,20},{28,24},{1,29},{... | collective-permute-start | bytes 196616 | tf_op jit(solution)/shard_map/ppermute | solution.py:30
  59.5 13.3 %quad_gather.1 = (bf16[1024,32]{1,0:T(8,128)(2,1)}, bf16[8,1024,128]{2,1,0:T(8,128)(2,1)}) custom-call(s32[8192]{0:T(1024)} %bitcast.249, bf16[64,32,128]{2,1,0:T(8,128)(2,1)} %get-tuple-element.130.basis_ref, bf16[8,128,32]{2,1,0:T(8,128)(2,1)} %bitcast.226, bf16[768,128]{1,0:T(8,128)(2,1)} %copy-done.102, bf16[768,128]{1,0:T(8,128)(2,1)} %copy-done.106, ...), custom_call_target="tpu_custom_call" | custom-call | flops 20000000000 | bytes 10000000 | tf_op jit(solution)/shard_map/quad_gather/pallas_call | solution.py:199
  75.3 17.6 %trip_gather.1 = (bf16[1024,64]{1,0:T(8,128)(2,1)}, bf16[8,1024,128]{2,1,0:T(8,128)(2,1)}) custom-call(s32[16384]{0:T(1024)} %bitcast.219, bf16[64,16,256]{2,1,0:T(8,128)(2,1)} %get-tuple-element.135.basis_ref, bf16[8,128,64]{2,1,0:T(8,128)(2,1)} %bitcast.228, bf16[768,128]{1,0:T(8,128)(2,1)} %copy-done.102, bf16[768,128]{1,0:T(8,128)(2,1)} %copy-done.106, ...), custom_call_target="tpu_custom_call" | custom-call | flops 20000000000 | bytes 10000000 | tf_op jit(solution)/shard_map/trip_gather/pallas_call | solution.py:199
  97.3 3.1 %multiply_add_fusion = (f32[1024,512]{1,0:T(8,128)S(1)}, f32[1024,512]{1,0:T(8,128)}) fusion(f32[1024,512]{1,0:T(8,128)S(1)} %fusion.135, f32[1024,512]{1,0:T(8,128)S(1)} %fusion.134, bf16[1024,128]{1,0:T(8,128)(2,1)S(1)} %copy-done.65, bf16[1024,128]{1,0:T(8,128)(2,1)S(1)} %copy-done.62, bf16[1024,128]{1,0:T(8,128)(2,1)S(1)} %copy-done.59, ...), kind=kOutput, calls=%fused_computation.11 | convolution fusion | flops 551026688 | bytes 11010048 | tf_op jit(solution)/shard_map/dot_general | solution.py:71
  111.4 3.0 %collective-permute-done.26 = f32[128,256]{1,0:T(8,128)S(1)} collective-permute-done((f32[128,256]{1,0:T(8,128)S(1)}, f32[128,256]{1,0:T(8,128)S(1)}, u32[]{:S(2)}, u32[]{:S(2)}) %collective-permute-start.26) | collective-permute-done | bytes 131104 | tf_op jit(solution)/shard_map/ppermute | solution.py:20
  122.5 2.7 multiply_convert_fusion.4
  130.4 3.5 %multiply_convert_fusion = (bf16[1024,512]{1,0:T(8,128)(2,1)S(1)}, bf16[1024,512]{1,0:T(8,128)(2,1)S(1)}, bf16[1024,512]{1,0:T(8,128)(2,1)S(1)}, f32[1024,512]{1,0:T(8,128)}) fusion(f32[1024,512]{1,0:T(8,128)S(1)} %copy-done.124, f32[1024,512]{1,0:T(8,128)S(1)} %copy-done.19, f32[1024,512]{1,0:T(8,128)S(1)} %copy-done.17, ...), kind=kOutput, calls=%fused_computation.1 | convolution fusion | flops 551550976 | bytes 15204352 | tf_op jit(solution)/shard_map/dot_general | solution.py:81
  138.3 3.0 %fusion.4 = f32[384,256]{1,0:T(8,128)} fusion(bf16[1024,512]{1,0:T(8,128)(2,1)} %copy-done.22, s32[1024]{0:T(1024)S(1)} %get-tuple-element.397, bf16[512,512]{1,0:T(8,128)(2,1)S(1)} %get-tuple-element.149), kind=kOutput, calls=%fused_computation.29 | convolution fusion | flops 503906304 | bytes 1708032 | tf_op jit(solution)/shard_map/dot_general | solution.py:81
  147.4 2.5 fusion.6
  162.0 30.3 %trip_scatter.1 = (bf16[3,512,128]{2,1,0:T(8,128)(2,1)}, bf16[3,512,128]{2,1,0:T(8,128)(2,1)}, bf16[3,512,128]{2,1,0:T(8,128)(2,1)}, bf16[3,512,128]{2,1,0:T(8,128)(2,1)}) custom-call(s32[16384]{0:T(1024)} %bitcast.220, f32[16384]{0:T(1024)} %fusion.59.same_ref, bf16[64,16,256]{2,1,0:T(8,128)(2,1)} %get-tuple-element.135.basis_ref, ...), custom_call_target="tpu_custom_call" | custom-call | flops 20000000000 | bytes 10000000 | tf_op jit(solution)/shard_map/trip_scatter/pallas_call | solution.py:404
  197.2 25.4 %quad_scatter.1 = (bf16[3,256,128]{2,1,0:T(8,128)(2,1)}, bf16[3,256,128]{2,1,0:T(8,128)(2,1)}, bf16[3,256,128]{2,1,0:T(8,128)(2,1)}, bf16[3,256,128]{2,1,0:T(8,128)(2,1)}) custom-call(s32[8192]{0:T(1024)} %bitcast.250, f32[8192]{0:T(1024)} %fusion.84.same_ref, bf16[64,32,128]{2,1,0:T(8,128)(2,1)} %get-tuple-element.130.basis_ref, ...), custom_call_target="tpu_custom_call" | custom-call | flops 20000000000 | bytes 10000000 | tf_op jit(solution)/shard_map/quad_scatter/pallas_call | solution.py:404
  227.1 2.5 collective-permute-done.51
  229.7 3.7 %collective-permute-start.52 = (bf16[304,128]{1,0:T(8,128)(2,1)S(1)}, bf16[304,128]{1,0:T(8,128)(2,1)S(1)}, u32[]{:S(2)}, u32[]{:S(2)}) collective-permute-start(bf16[304,128]{1,0:T(8,128)(2,1)S(1)} %broadcast_select_fusion.46), channel_id=1, source_target_pairs={{0,16},{4,20},{8,24},{12,28},{16,0},{20,4},{24,8},{28,12},{1,17},{... | collective-permute-start | bytes 233480 | tf_op jit(solution)/shard_map/ppermute | solution.py:25
  234.7 4.6 %collective-permute-start.40 = (bf16[1024,128]{1,0:T(8,128)(2,1)S(1)}, bf16[1024,128]{1,0:T(8,128)(2,1)S(1)}, u32[]{:S(2)}, u32[]{:S(2)}) collective-permute-start(bf16[1024,128]{1,0:T(8,128)(2,1)S(1)} %get-tuple-element.270), channel_id=1, source_target_pairs={{0,28},{4,0},{8,4},{12,8},{16,12},{20,16},{24,20},{28,24},{1,29},{... | collective-permute-start | bytes 786440 | tf_op jit(solution)/shard_map/ppermute | solution.py:30
  239.4 2.6 collective-permute-start.53
  242.1 8.0 %collective-permute-done.53 = bf16[304,128]{1,0:T(8,128)(2,1)S(1)} collective-permute-done((bf16[304,128]{1,0:T(8,128)(2,1)S(1)}, bf16[304,128]{1,0:T(8,128)(2,1)S(1)}, u32[]{:S(2)}, u32[]{:S(2)}) %collective-permute-start.53) | collective-permute-done | bytes 77856 | tf_op jit(solution)/shard_map/ppermute | solution.py:25
  260.8 2.7 collective-permute-start.48
  266.2 3.3 %collective-permute-done.49 = bf16[128,128]{1,0:T(8,128)(2,1)S(1)} collective-permute-done((bf16[128,128]{1,0:T(8,128)(2,1)S(1)}, bf16[128,128]{1,0:T(8,128)(2,1)S(1)}, u32[]{:S(2)}, u32[]{:S(2)}) %collective-permute-start.49) | collective-permute-done | bytes 32800 | tf_op jit(solution)/shard_map/ppermute | solution.py:25
  (582 shorter events, 121.4 us)
Async XLA Ops:
  7.4 14.2 %collective-permute-start.1 = (bf16[1024,128]{1,0:T(8,128)(2,1)S(1)}, bf16[1024,128]{1,0:T(8,128)(2,1)S(1)}, u32[]{:S(2)}, u32[]{:S(2)}) collective-permute-start(bf16[1024,128]{1,0:T(8,128)(2,1)S(1)} %get-tuple-element.114), channel_id=1, source_target_pairs={{0,2},{1,3},{2,0},{3,1},{4,6},{5,7},{6,4},{7,5},{8,10},{9,11},{10,... | collective-permute-start | bytes 786440 | tf_op jit(solution)/shard_map/ppermute | solution.py:20
  25.8 16.0 %collective-permute-start.17 = (bf16[768,128]{1,0:T(8,128)(2,1)S(1)}, bf16[768,128]{1,0:T(8,128)(2,1)S(1)}, u32[]{:S(2)}, u32[]{:S(2)}) collective-permute-start(bf16[768,128]{1,0:T(8,128)(2,1)S(1)} %maximum_maximum_fusion.2.refs_4_), channel_id=1, source_target_pairs={{0,28},{4,0},{8,4},{12,8},{16,12},{20,16},{24,20},{28,24},{1,29},{... | collective-permute-start | bytes 589832 | tf_op jit(solution)/shard_map/ppermute | solution.py:30
  44.1 14.0 %collective-permute-start.11 = (bf16[768,128]{1,0:T(8,128)(2,1)S(1)}, bf16[768,128]{1,0:T(8,128)(2,1)S(1)}, u32[]{:S(2)}, u32[]{:S(2)}) collective-permute-start(bf16[768,128]{1,0:T(8,128)(2,1)S(1)} %collective-permute-done.10.refs_0_), channel_id=1, source_target_pairs={{0,1},{1,0},{2,3},{3,2},{4,5},{5,4},{6,7},{7,6},{8,9},{9,8},{10,11... | collective-permute-start | bytes 589832 | tf_op jit(solution)/shard_map/ppermute | solution.py:20
  53.5 19.4 %collective-permute-start.9 = (bf16[128,256]{1,0:T(8,128)(2,1)S(1)}, bf16[128,256]{1,0:T(8,128)(2,1)S(1)}, u32[]{:S(2)}, u32[]{:S(2)}) collective-permute-start(bf16[128,256]{1,0:T(8,128)(2,1)S(1)} %get-tuple-element.364.refs_13_), channel_id=1, source_target_pairs={{0,28},{4,0},{8,4},{12,8},{16,12},{20,16},{24,20},{28,24},{1,29},{... | collective-permute-start | bytes 196616 | tf_op jit(solution)/shard_map/ppermute | solution.py:30
  58.0 14.9 %collective-permute-start.8 = (bf16[128,256]{1,0:T(8,128)(2,1)S(1)}, bf16[128,256]{1,0:T(8,128)(2,1)S(1)}, u32[]{:S(2)}, u32[]{:S(2)}) collective-permute-start(bf16[128,256]{1,0:T(8,128)(2,1)S(1)} %get-tuple-element.364.refs_13_), channel_id=1, source_target_pairs={{0,4},{4,8},{8,12},{12,16},{16,20},{20,24},{24,28},{28,0},{1,5},{5... | collective-permute-start | bytes 196616 | tf_op jit(solution)/shard_map/ppermute | solution.py:30
  58.1 14.9 %collective-permute-start.7 = (bf16[1888,128]{1,0:T(8,128)(2,1)S(1)}, bf16[1888,128]{1,0:T(8,128)(2,1)S(1)}, u32[]{:S(2)}, u32[]{:S(2)}) collective-permute-start(bf16[1888,128]{1,0:T(8,128)(2,1)S(1)} %constant_dynamic-update-slice_fusion.27.refs_12_.refs_0_), channel_id=1, source_target_pairs={{0,1},{1,0},{2,3},{3,2},{4,5},{5,4},{6,7},{7,6},{8,9},{9,8},{10,11... | collective-permute-start | bytes 1449992 | tf_op jit(solution)/shard_map/ppermute | solution.py:20
  58.3 14.6 %collective-permute-start.6 = (bf16[1888,128]{1,0:T(8,128)(2,1)S(1)}, bf16[1888,128]{1,0:T(8,128)(2,1)S(1)}, u32[]{:S(2)}, u32[]{:S(2)}) collective-permute-start(bf16[1888,128]{1,0:T(8,128)(2,1)S(1)} %constant_dynamic-update-slice_fusion.27.refs_12_.refs_0_), channel_id=1, source_target_pairs={{0,2},{1,3},{2,0},{3,1},{4,6},{5,7},{6,4},{7,5},{8,10},{9,11},{10,... | collective-permute-start | bytes 1449992 | tf_op jit(solution)/shard_map/ppermute | solution.py:20
  73.0 21.5 %collective-permute-start.22 = (bf16[1024,128]{1,0:T(8,128)(2,1)S(1)}, bf16[1024,128]{1,0:T(8,128)(2,1)S(1)}, u32[]{:S(2)}, u32[]{:S(2)}) collective-permute-start(bf16[1024,128]{1,0:T(8,128)(2,1)S(1)} %copy-done.48), channel_id=1, source_target_pairs={{0,1},{1,0},{2,3},{3,2},{4,5},{5,4},{6,7},{7,6},{8,9},{9,8},{10,11... | collective-permute-start | bytes 786440 | tf_op jit(solution)/shard_map/ppermute | solution.py:20
  73.1 21.4 %collective-permute-start.23 = (bf16[1024,128]{1,0:T(8,128)(2,1)S(1)}, bf16[1024,128]{1,0:T(8,128)(2,1)S(1)}, u32[]{:S(2)}, u32[]{:S(2)}) collective-permute-start(bf16[1024,128]{1,0:T(8,128)(2,1)S(1)} %copy-done.47), channel_id=1, source_target_pairs={{0,2},{1,3},{2,0},{3,1},{4,6},{5,7},{6,4},{7,5},{8,10},{9,11},{10,... | collective-permute-start | bytes 786440 | tf_op jit(solution)/shard_map/ppermute | solution.py:20
  74.6 19.9 %collective-permute-start.24 = (bf16[1024,128]{1,0:T(8,128)(2,1)S(1)}, bf16[1024,128]{1,0:T(8,128)(2,1)S(1)}, u32[]{:S(2)}, u32[]{:S(2)}) collective-permute-start(bf16[1024,128]{1,0:T(8,128)(2,1)S(1)} %copy-done.46), channel_id=1, source_target_pairs={{0,3},{1,2},{2,1},{3,0},{4,7},{5,6},{6,5},{7,4},{8,11},{9,10},{10,... | collective-permute-start | bytes 786440 | tf_op jit(solution)/shard_map/ppermute | solution.py:20
  74.9 19.6 %collective-permute-start.21 = (bf16[1888,128]{1,0:T(8,128)(2,1)S(1)}, bf16[1888,128]{1,0:T(8,128)(2,1)S(1)}, u32[]{:S(2)}, u32[]{:S(2)}) collective-permute-start(bf16[1888,128]{1,0:T(8,128)(2,1)S(1)} %collective-permute-done.6.refs_12_.refs_2_), channel_id=1, source_target_pairs={{0,1},{1,0},{2,3},{3,2},{4,5},{5,4},{6,7},{7,6},{8,9},{9,8},{10,11... | collective-permute-start | bytes 1449992 | tf_op jit(solution)/shard_map/ppermute | solution.py:20
  144.7 14.8 %collective-permute-start.29 = (bf16[1024,128]{1,0:T(8,128)(2,1)S(1)}, bf16[1024,128]{1,0:T(8,128)(2,1)}, u32[]{:S(2)}, u32[]{:S(2)}) collective-permute-start(bf16[1024,128]{1,0:T(8,128)(2,1)S(1)} %get-tuple-element.250.refs_12_), channel_id=1, source_target_pairs={{0,3},{1,2},{2,1},{3,0},{4,7},{5,6},{6,5},{7,4},{8,11},{9,10},{10,... | collective-permute-start | bytes 786440 | tf_op jit(solution)/shard_map/ppermute | solution.py:20
  145.4 14.4 %collective-permute-start.28 = (bf16[1024,128]{1,0:T(8,128)(2,1)S(1)}, bf16[1024,128]{1,0:T(8,128)(2,1)}, u32[]{:S(2)}, u32[]{:S(2)}) collective-permute-start(bf16[1024,128]{1,0:T(8,128)(2,1)S(1)} %get-tuple-element.251.refs_11_), channel_id=1, source_target_pairs={{0,2},{1,3},{2,0},{3,1},{4,6},{5,7},{6,4},{7,5},{8,10},{9,11},{10,... | collective-permute-start | bytes 786440 | tf_op jit(solution)/shard_map/ppermute | solution.py:20
  157.7 36.6 %collective-permute-start.30 = (bf16[2848,128]{1,0:T(8,128)(2,1)}, bf16[2848,128]{1,0:T(8,128)(2,1)S(1)}, u32[]{:S(2)}, u32[]{:S(2)}) collective-permute-start(bf16[2848,128]{1,0:T(8,128)(2,1)} %get-tuple-element.167.refs_2_), channel_id=1, source_target_pairs={{0,1},{1,0},{2,3},{3,2},{4,5},{5,4},{6,7},{7,6},{8,9},{9,8},{10,11... | collective-permute-start | bytes 2187272 | tf_op jit(solution)/shard_map/ppermute | solution.py:20
  158.0 36.4 %collective-permute-start.31 = (bf16[2848,128]{1,0:T(8,128)(2,1)S(1)}, bf16[2848,128]{1,0:T(8,128)(2,1)}, u32[]{:S(2)}, u32[]{:S(2)}) collective-permute-start(bf16[2848,128]{1,0:T(8,128)(2,1)S(1)} %get-tuple-element.168.refs_3_), channel_id=1, source_target_pairs={{0,2},{1,3},{2,0},{3,1},{4,6},{5,7},{6,4},{7,5},{8,10},{9,11},{10,... | collective-permute-start | bytes 2187272 | tf_op jit(solution)/shard_map/ppermute | solution.py:20
  159.5 34.9 %collective-permute-start.32 = (bf16[2848,128]{1,0:T(8,128)(2,1)S(1)}, bf16[2848,128]{1,0:T(8,128)(2,1)}, u32[]{:S(2)}, u32[]{:S(2)}) collective-permute-start(bf16[2848,128]{1,0:T(8,128)(2,1)S(1)} %get-tuple-element.169.refs_4_), channel_id=1, source_target_pairs={{0,3},{1,2},{2,1},{3,0},{4,7},{5,6},{6,5},{7,4},{8,11},{9,10},{10,... | collective-permute-start | bytes 2187272 | tf_op jit(solution)/shard_map/ppermute | solution.py:20
  192.4 30.3 %collective-permute-start.34 = (bf16[3,512,128]{2,1,0:T(8,128)(2,1)}, bf16[3,512,128]{2,1,0:T(8,128)(2,1)}, u32[]{:S(2)}, u32[]{:S(2)}) collective-permute-start(bf16[3,512,128]{2,1,0:T(8,128)(2,1)} %get-tuple-element.176.refs_3_), channel_id=1, source_target_pairs={{0,1},{1,0},{2,3},{3,2},{4,5},{5,4},{6,7},{7,6},{8,9},{9,8},{10,11... | collective-permute-start | bytes 1179656 | tf_op jit(solution)/shard_map/ppermute | solution.py:20
  192.9 29.8 %collective-permute-start.35 = (bf16[3,512,128]{2,1,0:T(8,128)(2,1)}, bf16[3,512,128]{2,1,0:T(8,128)(2,1)}, u32[]{:S(2)}, u32[]{:S(2)}) collective-permute-start(bf16[3,512,128]{2,1,0:T(8,128)(2,1)} %get-tuple-element.177.refs_4_), channel_id=1, source_target_pairs={{0,2},{1,3},{2,0},{3,1},{4,6},{5,7},{6,4},{7,5},{8,10},{9,11},{10,... | collective-permute-start | bytes 1179656 | tf_op jit(solution)/shard_map/ppermute | solution.py:20
  194.3 28.4 %collective-permute-start.36 = (bf16[3,512,128]{2,1,0:T(8,128)(2,1)}, bf16[3,512,128]{2,1,0:T(8,128)(2,1)}, u32[]{:S(2)}, u32[]{:S(2)}) collective-permute-start(bf16[3,512,128]{2,1,0:T(8,128)(2,1)} %get-tuple-element.178.refs_5_), channel_id=1, source_target_pairs={{0,3},{1,2},{2,1},{3,0},{4,7},{5,6},{6,5},{7,4},{8,11},{9,10},{10,... | collective-permute-start | bytes 1179656 | tf_op jit(solution)/shard_map/ppermute | solution.py:20
  196.3 26.4 %collective-permute-start.33 = (bf16[1216,128]{1,0:T(8,128)(2,1)S(1)}, bf16[1216,128]{1,0:T(8,128)(2,1)S(1)}, u32[]{:S(2)}, u32[]{:S(2)}) collective-permute-start(bf16[1216,128]{1,0:T(8,128)(2,1)S(1)} %broadcast_select_fusion.2.refs_1_), channel_id=1, source_target_pairs={{0,4},{4,0},{8,12},{12,8},{16,20},{20,16},{24,28},{28,24},{1,5},{5... | collective-permute-start | bytes 933896 | tf_op jit(solution)/shard_map/ppermute | solution.py:25
  234.7 16.2 %collective-permute-start.40 = (bf16[1024,128]{1,0:T(8,128)(2,1)S(1)}, bf16[1024,128]{1,0:T(8,128)(2,1)S(1)}, u32[]{:S(2)}, u32[]{:S(2)}) collective-permute-start(bf16[1024,128]{1,0:T(8,128)(2,1)S(1)} %get-tuple-element.270), channel_id=1, source_target_pairs={{0,28},{4,0},{8,4},{12,8},{16,12},{20,16},{24,20},{28,24},{1,29},{... | collective-permute-start | bytes 786440 | tf_op jit(solution)/shard_map/ppermute | solution.py:30
  250.2 15.9 %collective-permute-start.54 = (bf16[608,128]{1,0:T(8,128)(2,1)S(1)}, bf16[608,128]{1,0:T(8,128)(2,1)S(1)}, u32[]{:S(2)}, u32[]{:S(2)}) collective-permute-start(bf16[608,128]{1,0:T(8,128)(2,1)S(1)} %pad_maximum_fusion.14), channel_id=1, source_target_pairs={{0,8},{4,12},{8,0},{12,4},{16,24},{20,28},{24,16},{28,20},{1,9},{5... | collective-permute-start | bytes 466952 | tf_op jit(solution)/shard_map/ppermute | solution.py:25
  263.6 14.8 %collective-permute-start.44 = (bf16[1024,128]{1,0:T(8,128)(2,1)S(1)}, bf16[1024,128]{1,0:T(8,128)(2,1)S(1)}, u32[]{:S(2)}, u32[]{:S(2)}) collective-permute-start(bf16[1024,128]{1,0:T(8,128)(2,1)S(1)} %get-tuple-element.235), channel_id=1, source_target_pairs={{0,1},{1,0},{2,3},{3,2},{4,5},{5,4},{6,7},{7,6},{8,9},{9,8},{10,11... | collective-permute-start | bytes 786440 | tf_op jit(solution)/shard_map/ppermute | solution.py:20
  263.7 14.7 %collective-permute-start.43 = (bf16[1024,128]{1,0:T(8,128)(2,1)S(1)}, bf16[1024,128]{1,0:T(8,128)(2,1)S(1)}, u32[]{:S(2)}, u32[]{:S(2)}) collective-permute-start(bf16[1024,128]{1,0:T(8,128)(2,1)S(1)} %get-tuple-element.236), channel_id=1, source_target_pairs={{0,2},{1,3},{2,0},{3,1},{4,6},{5,7},{6,4},{7,5},{8,10},{9,11},{10,... | collective-permute-start | bytes 786440 | tf_op jit(solution)/shard_map/ppermute | solution.py:20
  (160 other events, 996.2 us)
where the time goes:
time: 291 us; the launch traced here: 289 us
  Pallas kernels  94.6 us (33%)
  starting transfers between devices  56.1 us (19%)
  matrix products  45.8 us (16%)
  waiting for transfers between devices  37.6 us (13%)
  local copies, waits for them, and re-layouts  26.3 us (9%)
  other arithmetic  25.7 us (9%)
  between operations  3 us (1%)
    pallas_call x2, Pallas kernels, branch_backward(): pl.pallas_call(functools.partial(scatter_body, folds=folds, owners=owners...  55.7 us
    pallas_call x2, Pallas kernels, branch_forward(): pl.pallas_call(functools.partial(gather_body, folds=folds, first_row=firs...  30.9 us
    ppermute x44, starting transfers between devices, chan_swap(): return lax.ppermute(value, 'chan', [(i, i ^ mask) for i in range(count)])  28.1 us
    ppermute x44, waiting for transfers between devices, chan_swap(): return lax.ppermute(value, 'chan', [(i, i ^ mask) for i in range(count)])  21.9 us
    dot_general x15, matrix products, matmul(): return jnp.dot(first_op, second_op, preferred_element_type=F32)  17 us
    dot_general x9, matrix products, outer(): lax.dot_general(first_op, second_op, (((1,), (1,)), ((), ())), preferred_...  16.4 us
    ppermute x9, waiting for transfers between devices, edge_swap(): return lax.ppermute(value, 'edge', [(i, i ^ mask) for i in range(count)])  15.5 us
    ppermute x9, starting transfers between devices, edge_swap(): return lax.ppermute(value, 'edge', [(i, i ^ mask) for i in range(count)])  14.1 us
  transfers between devices with their start and end apart: 59, of which 13 were waited for; matrix products, arithmetic and copies ran while one was open for 15% of the time, Pallas kernels for 33%

commit v1 on v0

--- a/solution.py
+++ b/solution.py
@@ -694,6 +694,11 @@
         atom_emb,
         grad_edges,
     )
+    tag_onehot = (atom_tags[:, None] == jnp.arange(TAGS)[None, :]).astype(F32)
+    atom_full = atom_emb.astype(F32) + jnp.dot(
+        tag_onehot, tag_table.astype(F32), precision=HIGHEST
+    )
+    atom_low = atom_full.astype(BF16)
     before = edge_shift(wire, 1)
     later = edge_shift(wire, -1)
     own_across = chan_swap(wire, 2)
@@ -704,6 +709,9 @@
 
     before_across = chan_swap(before, 2)
     later_across = chan_swap(later, 2)
+    before_across, later_across, atom_before, atom_later = gate(
+        before_across, later_across, edge_shift(atom_low, 1), edge_shift(atom_low, -1)
+    )
     wire_pieces = (
         spread(before, before_across)
         + [wire, own_beside, own_across, chan_swap(own_across, 1)]
@@ -723,11 +731,6 @@
     )
 
     large = jnp.concatenate(members[:5] + [columns(members[5]), columns(members[6])], axis=0)
-    tag_onehot = (atom_tags[:, None] == jnp.arange(TAGS)[None, :]).astype(F32)
-    atom_full = atom_emb.astype(F32) + jnp.dot(
-        tag_onehot, tag_table.astype(F32), precision=HIGHEST
-    )
-    atom_low = atom_full.astype(BF16)
     grad_blocks = grad_edges.reshape(parts, edges, cols)
     grad_sent = [pick(grad_blocks, rank ^ step) for step in range(parts)]
     quad_agg, quad_sum = branch_forward(
@@ -736,14 +739,12 @@
         trip_rows,
         quad_basis,
         quad_bil,
-        [large, atom_low] + grad_sent,
+        [large] + grad_sent,
         "quad_gather",
     )
-    large_across, large_beside, atom_before, atom_later, quad_agg, *grad_sent = gate(
+    large_across, large_beside, quad_agg, *grad_sent = gate(
         chan_swap(large, 2),
         chan_swap(large, 1),
-        edge_shift(atom_low, 1),
-        edge_shift(atom_low, -1),
         quad_agg,
         *grad_sent,
     )
@@ -754,7 +755,7 @@
         0,
         trip_basis,
         trip_bil,
-        [large_across, atom_before, atom_later] + grad_sent,
+        [large_across] + grad_sent,
         "trip_gather",
     )
     grad_got = [grad_sent[0]] + [chan_swap(grad_sent[step], step) for step in range(1, parts)]

time: 291 us -> 290 us (level)
  starting transfers between devices: 56.1 us -> 50.1 us
  waiting for transfers between devices: 37.6 us -> 40.7 us
    ppermute x6, waiting for transfers between devices: 0.25 us -> 6.07 us  [edge_shift(): lax.ppermute(value, 'edge', [(i, (i + step) % count) for i in range(count)])]
    ppermute x9, starting transfers between devices: 14.1 us -> 10.1 us  [edge_swap(): return lax.ppermute(value, 'edge', [(i, i ^ mask) for i in range(count)])]
    ppermute x44, waiting for transfers between devices: 21.9 us -> 18.2 us  [chan_swap(): return lax.ppermute(value, 'chan', [(i, i ^ mask) for i in range(count)])]
    unnamed x305 -> x289, local copies, waits for them, and re-layouts: 10.5 us -> 11.8 us
  transfers between devices with their start and end apart: 59 -> 59, of which waited for: 13 -> 16; matrix products, arithmetic and copies ran while one was open for 15% -> 16% of each run, Pallas kernels for 33% -> 33%
where the time goes in v1:
time: 290 us; the launch traced here: 288 us
  Pallas kernels  94.8 us (33%)
  starting transfers between devices  50.1 us (17%)
  matrix products  46.6 us (16%)
  waiting for transfers between devices  40.7 us (14%)
  local copies, waits for them, and re-layouts  27.7 us (10%)
  other arithmetic  25.6 us (9%)
    pallas_call x2, Pallas kernels, branch_backward(): pl.pallas_call(functools.partial(scatter_body, folds=folds, owners=owners...  55.8 us
    pallas_call x2, Pallas kernels, branch_forward(): pl.pallas_call(functools.partial(gather_body, folds=folds, first_row=firs...  30.9 us
    ppermute x44, starting transfers between devices, chan_swap(): return lax.ppermute(value, 'chan', [(i, i ^ mask) for i in range(count)])  28.6 us
    ppermute x44, waiting for transfers between devices, chan_swap(): return lax.ppermute(value, 'chan', [(i, i ^ mask) for i in range(count)])  18.2 us
    dot_general x15, matrix products, matmul(): return jnp.dot(first_op, second_op, preferred_element_type=F32)  17.8 us
    ppermute x9, waiting for transfers between devices, edge_swap(): return lax.ppermute(value, 'edge', [(i, i ^ mask) for i in range(count)])  16.4 us
    dot_general x9, matrix products, outer(): lax.dot_general(first_op, second_op, (((1,), (1,)), ((), ())), preferred_...  16.4 us
    unnamed x289, local copies, waits for them, and re-layouts  11.8 us
  transfers between devices with their start and end apart: 59, of which 16 were waited for; matrix products, arithmetic and copies ran while one was open for 16% of the time, Pallas kernels for 33%

profile of v1, /device:TPU:0, one launch (start us, length us, event | category | flops | bytes accessed | tf_op | source)
XLA Modules:
  0.0 288.3 jit_solution(8859199166644739261)
XLA Ops:
  3.1 2.6 collective-permute-start.4
  15.8 5.8 %collective-permute-done.1 = bf16[1024,128]{1,0:T(8,128)(2,1)S(1)} collective-permute-done((bf16[1024,128]{1,0:T(8,128)(2,1)S(1)}, bf16[1024,128]{1,0:T(8,128)(2,1)S(1)}, u32[]{:S(2)}, u32[]{:S(2)}) %collective-permute-start.1) | collective-permute-done | bytes 262176 | tf_op jit(solution)/shard_map/ppermute | solution.py:20
  27.6 4.5 %collective-permute-start.11 = (bf16[768,128]{1,0:T(8,128)(2,1)S(1)}, bf16[768,128]{1,0:T(8,128)(2,1)}, u32[]{:S(2)}, u32[]{:S(2)}) collective-permute-start(bf16[768,128]{1,0:T(8,128)(2,1)S(1)} %maximum_maximum_fusion.2.refs_4_), channel_id=1, source_target_pairs={{0,28},{4,0},{8,4},{12,8},{16,12},{20,16},{24,20},{28,24},{1,29},{... | collective-permute-start | bytes 589832 | tf_op jit(solution)/shard_map/ppermute | solution.py:30
  33.0 4.7 %collective-permute-start.14 = (bf16[128,256]{1,0:T(8,128)(2,1)S(1)}, bf16[128,256]{1,0:T(8,128)(2,1)}, u32[]{:S(2)}, u32[]{:S(2)}) collective-permute-start(bf16[128,256]{1,0:T(8,128)(2,1)S(1)} %get-tuple-element.368), channel_id=1, source_target_pairs={{0,28},{4,0},{8,4},{12,8},{16,12},{20,16},{24,20},{28,24},{1,29},{... | collective-permute-start | bytes 196616 | tf_op jit(solution)/shard_map/ppermute | solution.py:30
  39.2 6.4 %slot_basis.1 = (bf16[64,16,256]{2,1,0:T(8,128)(2,1)}, bf16[64,32,128]{2,1,0:T(8,128)(2,1)}) custom-call(s32[1]{0:T(128)} %bitcast.20.rank_ref, bf16[16,16,4096]{2,1,0:T(8,128)(2,1)} %trip_vals.1, s32[16,4096]{1,0:T(8,128)} %trip_keep.1, bf16[32,8,4096]{2,1,0:T(8,128)(2,1)} %quad_vals.1, s32[8,4096]{1,0:T(8,128)} %quad_keep.1), custom_call_target="tpu_custom_call" | custom-call | flops 10000000000 | bytes 10000000 | tf_op jit(solution)/shard_map/slot_basis/pallas_call | solution.py:269
  48.9 5.8 %collective-permute-done.13 = bf16[128,256]{1,0:T(8,128)(2,1)S(1)} collective-permute-done((bf16[128,256]{1,0:T(8,128)(2,1)S(1)}, bf16[128,256]{1,0:T(8,128)(2,1)S(1)}, u32[]{:S(2)}, u32[]{:S(2)}) %collective-permute-start.13) | collective-permute-done | bytes 65568 | tf_op jit(solution)/shard_map/ppermute | solution.py:30
  57.1 2.4 fusion.2
  60.9 13.4 %quad_gather.1 = (bf16[1024,32]{1,0:T(8,128)(2,1)}, bf16[8,1024,128]{2,1,0:T(8,128)(2,1)}) custom-call(s32[8192]{0:T(1024)} %bitcast.249, bf16[64,32,128]{2,1,0:T(8,128)(2,1)} %get-tuple-element.131.basis_ref, bf16[8,128,32]{2,1,0:T(8,128)(2,1)} %bitcast.226, bf16[768,128]{1,0:T(8,128)(2,1)} %collective-permute-done.8.refs_0_, bf16[768,128]{1,0:T(8,128)(2,1)} %copy-done.101, ...), custom_call_target="tpu_custom_call" | custom-call | flops 20000000000 | bytes 10000000 | tf_op jit(solution)/shard_map/quad_gather/pallas_call | solution.py:199
  76.6 17.5 %trip_gather.1 = (bf16[1024,64]{1,0:T(8,128)(2,1)}, bf16[8,1024,128]{2,1,0:T(8,128)(2,1)}) custom-call(s32[16384]{0:T(1024)} %bitcast.219, bf16[64,16,256]{2,1,0:T(8,128)(2,1)} %get-tuple-element.139.basis_ref, bf16[8,128,64]{2,1,0:T(8,128)(2,1)} %bitcast.228, bf16[768,128]{1,0:T(8,128)(2,1)} %collective-permute-done.8.refs_0_, ...), custom_call_target="tpu_custom_call" | custom-call | flops 20000000000 | bytes 10000000 | tf_op jit(solution)/shard_map/trip_gather/pallas_call | solution.py:199
  97.9 3.1 %multiply_add_fusion = (f32[1024,512]{1,0:T(8,128)S(1)}, f32[1024,512]{1,0:T(8,128)}) fusion(f32[1024,512]{1,0:T(8,128)S(1)} %fusion.135, f32[1024,512]{1,0:T(8,128)S(1)} %fusion.134, bf16[1024,128]{1,0:T(8,128)(2,1)S(1)} %copy-done.63, bf16[1024,128]{1,0:T(8,128)(2,1)S(1)} %copy-done.60, bf16[1024,128]{1,0:T(8,128)(2,1)S(1)} %copy-done.57, ...), kind=kOutput, calls=%fused_computation.11 | convolution fusion | flops 551026688 | bytes 11010048 | tf_op jit(solution)/shard_map/dot_general | solution.py:71
  111.9 3.2 %collective-permute-done.26 = f32[128,256]{1,0:T(8,128)S(1)} collective-permute-done((f32[128,256]{1,0:T(8,128)S(1)}, f32[128,256]{1,0:T(8,128)S(1)}, u32[]{:S(2)}, u32[]{:S(2)}) %collective-permute-start.26) | collective-permute-done | bytes 131104 | tf_op jit(solution)/shard_map/ppermute | solution.py:20
  120.1 2.3 slice_bitcast_fusion.10
  123.0 2.7 multiply_convert_fusion.4
  131.0 3.5 %multiply_convert_fusion = (bf16[1024,512]{1,0:T(8,128)(2,1)S(1)}, bf16[1024,512]{1,0:T(8,128)(2,1)S(1)}, bf16[1024,512]{1,0:T(8,128)(2,1)S(1)}, f32[1024,512]{1,0:T(8,128)}) fusion(f32[1024,512]{1,0:T(8,128)S(1)} %copy-done.116, f32[1024,512]{1,0:T(8,128)S(1)} %copy-done.19, f32[1024,512]{1,0:T(8,128)S(1)} %copy-done.17, ...), kind=kOutput, calls=%fused_computation.1 | convolution fusion | flops 551550976 | bytes 15204352 | tf_op jit(solution)/shard_map/dot_general | solution.py:81
  138.9 3.0 %fusion.4 = f32[384,256]{1,0:T(8,128)} fusion(bf16[1024,512]{1,0:T(8,128)(2,1)} %copy-done.22, s32[1024]{0:T(1024)S(1)} %get-tuple-element.401, bf16[512,512]{1,0:T(8,128)(2,1)S(1)} %get-tuple-element.153), kind=kOutput, calls=%fused_computation.29 | convolution fusion | flops 503906304 | bytes 1708032 | tf_op jit(solution)/shard_map/dot_general | solution.py:81
  148.0 2.5 fusion.6
  153.1 2.3 fusion.25.refs_6_
  162.6 30.3 %trip_scatter.1 = (bf16[3,512,128]{2,1,0:T(8,128)(2,1)}, bf16[3,512,128]{2,1,0:T(8,128)(2,1)}, bf16[3,512,128]{2,1,0:T(8,128)(2,1)}, bf16[3,512,128]{2,1,0:T(8,128)(2,1)}) custom-call(s32[16384]{0:T(1024)} %bitcast.220, f32[16384]{0:T(1024)} %fusion.59.same_ref, bf16[64,16,256]{2,1,0:T(8,128)(2,1)} %get-tuple-element.139.basis_ref, ...), custom_call_target="tpu_custom_call" | custom-call | flops 20000000000 | bytes 10000000 | tf_op jit(solution)/shard_map/trip_scatter/pallas_call | solution.py:404
  197.7 25.5 %quad_scatter.1 = (bf16[3,256,128]{2,1,0:T(8,128)(2,1)}, bf16[3,256,128]{2,1,0:T(8,128)(2,1)}, bf16[3,256,128]{2,1,0:T(8,128)(2,1)}, bf16[3,256,128]{2,1,0:T(8,128)(2,1)}) custom-call(s32[8192]{0:T(1024)} %bitcast.250, f32[8192]{0:T(1024)} %fusion.84.same_ref, bf16[64,32,128]{2,1,0:T(8,128)(2,1)} %get-tuple-element.131.basis_ref, ...), custom_call_target="tpu_custom_call" | custom-call | flops 20000000000 | bytes 10000000 | tf_op jit(solution)/shard_map/quad_scatter/pallas_call | solution.py:404
  227.7 2.5 collective-permute-done.51
  232.6 2.5 collective-permute-done.39
  237.5 2.4 collective-permute-start.53
  240.0 9.8 %collective-permute-done.53 = bf16[304,128]{1,0:T(8,128)(2,1)S(1)} collective-permute-done((bf16[304,128]{1,0:T(8,128)(2,1)S(1)}, bf16[304,128]{1,0:T(8,128)(2,1)S(1)}, u32[]{:S(2)}, u32[]{:S(2)}) %collective-permute-start.53) | collective-permute-done | bytes 77856 | tf_op jit(solution)/shard_map/ppermute | solution.py:25
  265.8 2.3 collective-permute-done.49
  (566 shorter events, 124.4 us)
Async XLA Ops:
  25.8 29.0 %collective-permute-start.17 = (bf16[768,128]{1,0:T(8,128)(2,1)S(1)}, bf16[768,128]{1,0:T(8,128)(2,1)S(1)}, u32[]{:S(2)}, u32[]{:S(2)}) collective-permute-start(bf16[768,128]{1,0:T(8,128)(2,1)S(1)} %maximum_maximum_fusion.2.refs_4_), channel_id=1, source_target_pairs={{0,2},{1,3},{2,0},{3,1},{4,6},{5,7},{6,4},{7,5},{8,10},{9,11},{10,... | collective-permute-start | bytes 589832 | tf_op jit(solution)/shard_map/ppermute | solution.py:20
  27.6 29.0 %collective-permute-start.16 = (bf16[768,128]{1,0:T(8,128)(2,1)S(1)}, bf16[768,128]{1,0:T(8,128)(2,1)}, u32[]{:S(2)}, u32[]{:S(2)}) collective-permute-start(bf16[768,128]{1,0:T(8,128)(2,1)S(1)} %maximum_maximum_fusion.2.refs_4_), channel_id=1, source_target_pairs={{0,1},{1,0},{2,3},{3,2},{4,5},{5,4},{6,7},{7,6},{8,9},{9,8},{10,11... | collective-permute-start | bytes 589832 | tf_op jit(solution)/shard_map/ppermute | solution.py:20
  27.6 18.0 %collective-permute-start.11 = (bf16[768,128]{1,0:T(8,128)(2,1)S(1)}, bf16[768,128]{1,0:T(8,128)(2,1)}, u32[]{:S(2)}, u32[]{:S(2)}) collective-permute-start(bf16[768,128]{1,0:T(8,128)(2,1)S(1)} %maximum_maximum_fusion.2.refs_4_), channel_id=1, source_target_pairs={{0,28},{4,0},{8,4},{12,8},{16,12},{20,16},{24,20},{28,24},{1,29},{... | collective-permute-start | bytes 589832 | tf_op jit(solution)/shard_map/ppermute | solution.py:30
  33.0 14.7 %collective-permute-start.14 = (bf16[128,256]{1,0:T(8,128)(2,1)S(1)}, bf16[128,256]{1,0:T(8,128)(2,1)}, u32[]{:S(2)}, u32[]{:S(2)}) collective-permute-start(bf16[128,256]{1,0:T(8,128)(2,1)S(1)} %get-tuple-element.368), channel_id=1, source_target_pairs={{0,28},{4,0},{8,4},{12,8},{16,12},{20,16},{24,20},{28,24},{1,29},{... | collective-permute-start | bytes 196616 | tf_op jit(solution)/shard_map/ppermute | solution.py:30
  59.4 14.8 %collective-permute-start.7 = (bf16[1888,128]{1,0:T(8,128)(2,1)S(1)}, bf16[1888,128]{1,0:T(8,128)(2,1)S(1)}, u32[]{:S(2)}, u32[]{:S(2)}) collective-permute-start(bf16[1888,128]{1,0:T(8,128)(2,1)S(1)} %constant_dynamic-update-slice_fusion.27.refs_12_.refs_0_), channel_id=1, source_target_pairs={{0,1},{1,0},{2,3},{3,2},{4,5},{5,4},{6,7},{7,6},{8,9},{9,8},{10,11... | collective-permute-start | bytes 1449992 | tf_op jit(solution)/shard_map/ppermute | solution.py:20
  59.5 14.7 %collective-permute-start.6 = (bf16[1888,128]{1,0:T(8,128)(2,1)S(1)}, bf16[1888,128]{1,0:T(8,128)(2,1)S(1)}, u32[]{:S(2)}, u32[]{:S(2)}) collective-permute-start(bf16[1888,128]{1,0:T(8,128)(2,1)S(1)} %constant_dynamic-update-slice_fusion.27.refs_12_.refs_0_), channel_id=1, source_target_pairs={{0,2},{1,3},{2,0},{3,1},{4,6},{5,7},{6,4},{7,5},{8,10},{9,11},{10,... | collective-permute-start | bytes 1449992 | tf_op jit(solution)/shard_map/ppermute | solution.py:20
  74.3 19.9 %collective-permute-start.22 = (bf16[1024,128]{1,0:T(8,128)(2,1)S(1)}, bf16[1024,128]{1,0:T(8,128)(2,1)S(1)}, u32[]{:S(2)}, u32[]{:S(2)}) collective-permute-start(bf16[1024,128]{1,0:T(8,128)(2,1)S(1)} %copy-done.48), channel_id=1, source_target_pairs={{0,1},{1,0},{2,3},{3,2},{4,5},{5,4},{6,7},{7,6},{8,9},{9,8},{10,11... | collective-permute-start | bytes 786440 | tf_op jit(solution)/shard_map/ppermute | solution.py:20
  74.5 19.7 %collective-permute-start.23 = (bf16[1024,128]{1,0:T(8,128)(2,1)S(1)}, bf16[1024,128]{1,0:T(8,128)(2,1)S(1)}, u32[]{:S(2)}, u32[]{:S(2)}) collective-permute-start(bf16[1024,128]{1,0:T(8,128)(2,1)S(1)} %copy-done.47), channel_id=1, source_target_pairs={{0,2},{1,3},{2,0},{3,1},{4,6},{5,7},{6,4},{7,5},{8,10},{9,11},{10,... | collective-permute-start | bytes 786440 | tf_op jit(solution)/shard_map/ppermute | solution.py:20
  76.0 18.2 %collective-permute-start.24 = (bf16[1024,128]{1,0:T(8,128)(2,1)S(1)}, bf16[1024,128]{1,0:T(8,128)(2,1)S(1)}, u32[]{:S(2)}, u32[]{:S(2)}) collective-permute-start(bf16[1024,128]{1,0:T(8,128)(2,1)S(1)} %copy-done.46), channel_id=1, source_target_pairs={{0,3},{1,2},{2,1},{3,0},{4,7},{5,6},{6,5},{7,4},{8,11},{9,10},{10,... | collective-permute-start | bytes 786440 | tf_op jit(solution)/shard_map/ppermute | solution.py:20
  76.2 18.0 %collective-permute-start.21 = (bf16[1888,128]{1,0:T(8,128)(2,1)S(1)}, bf16[1888,128]{1,0:T(8,128)(2,1)S(1)}, u32[]{:S(2)}, u32[]{:S(2)}) collective-permute-start(bf16[1888,128]{1,0:T(8,128)(2,1)S(1)} %collective-permute-done.6.refs_12_.refs_2_), channel_id=1, source_target_pairs={{0,1},{1,0},{2,3},{3,2},{4,5},{5,4},{6,7},{7,6},{8,9},{9,8},{10,11... | collective-permute-start | bytes 1449992 | tf_op jit(solution)/shard_map/ppermute | solution.py:20
  145.3 14.8 %collective-permute-start.29 = (bf16[1024,128]{1,0:T(8,128)(2,1)S(1)}, bf16[1024,128]{1,0:T(8,128)(2,1)}, u32[]{:S(2)}, u32[]{:S(2)}) collective-permute-start(bf16[1024,128]{1,0:T(8,128)(2,1)S(1)} %get-tuple-element.254.refs_12_), channel_id=1, source_target_pairs={{0,3},{1,2},{2,1},{3,0},{4,7},{5,6},{6,5},{7,4},{8,11},{9,10},{10,... | collective-permute-start | bytes 786440 | tf_op jit(solution)/shard_map/ppermute | solution.py:20
  146.1 14.3 %collective-permute-start.28 = (bf16[1024,128]{1,0:T(8,128)(2,1)S(1)}, bf16[1024,128]{1,0:T(8,128)(2,1)}, u32[]{:S(2)}, u32[]{:S(2)}) collective-permute-start(bf16[1024,128]{1,0:T(8,128)(2,1)S(1)} %get-tuple-element.255.refs_11_), channel_id=1, source_target_pairs={{0,2},{1,3},{2,0},{3,1},{4,6},{5,7},{6,4},{7,5},{8,10},{9,11},{10,... | collective-permute-start | bytes 786440 | tf_op jit(solution)/shard_map/ppermute | solution.py:20
  158.2 36.6 %collective-permute-start.30 = (bf16[2848,128]{1,0:T(8,128)(2,1)}, bf16[2848,128]{1,0:T(8,128)(2,1)S(1)}, u32[]{:S(2)}, u32[]{:S(2)}) collective-permute-start(bf16[2848,128]{1,0:T(8,128)(2,1)} %get-tuple-element.171.refs_2_), channel_id=1, source_target_pairs={{0,1},{1,0},{2,3},{3,2},{4,5},{5,4},{6,7},{7,6},{8,9},{9,8},{10,11... | collective-permute-start | bytes 2187272 | tf_op jit(solution)/shard_map/ppermute | solution.py:20
  158.5 36.4 %collective-permute-start.31 = (bf16[2848,128]{1,0:T(8,128)(2,1)S(1)}, bf16[2848,128]{1,0:T(8,128)(2,1)}, u32[]{:S(2)}, u32[]{:S(2)}) collective-permute-start(bf16[2848,128]{1,0:T(8,128)(2,1)S(1)} %get-tuple-element.172.refs_3_), channel_id=1, source_target_pairs={{0,2},{1,3},{2,0},{3,1},{4,6},{5,7},{6,4},{7,5},{8,10},{9,11},{10,... | collective-permute-start | bytes 2187272 | tf_op jit(solution)/shard_map/ppermute | solution.py:20
  160.0 34.9 %collective-permute-start.32 = (bf16[2848,128]{1,0:T(8,128)(2,1)S(1)}, bf16[2848,128]{1,0:T(8,128)(2,1)}, u32[]{:S(2)}, u32[]{:S(2)}) collective-permute-start(bf16[2848,128]{1,0:T(8,128)(2,1)S(1)} %get-tuple-element.173.refs_4_), channel_id=1, source_target_pairs={{0,3},{1,2},{2,1},{3,0},{4,7},{5,6},{6,5},{7,4},{8,11},{9,10},{10,... | collective-permute-start | bytes 2187272 | tf_op jit(solution)/shard_map/ppermute | solution.py:20
  192.9 30.4 %collective-permute-start.34 = (bf16[3,512,128]{2,1,0:T(8,128)(2,1)}, bf16[3,512,128]{2,1,0:T(8,128)(2,1)}, u32[]{:S(2)}, u32[]{:S(2)}) collective-permute-start(bf16[3,512,128]{2,1,0:T(8,128)(2,1)} %get-tuple-element.180.refs_3_), channel_id=1, source_target_pairs={{0,1},{1,0},{2,3},{3,2},{4,5},{5,4},{6,7},{7,6},{8,9},{9,8},{10,11... | collective-permute-start | bytes 1179656 | tf_op jit(solution)/shard_map/ppermute | solution.py:20
  193.5 29.8 %collective-permute-start.35 = (bf16[3,512,128]{2,1,0:T(8,128)(2,1)}, bf16[3,512,128]{2,1,0:T(8,128)(2,1)}, u32[]{:S(2)}, u32[]{:S(2)}) collective-permute-start(bf16[3,512,128]{2,1,0:T(8,128)(2,1)} %get-tuple-element.181.refs_4_), channel_id=1, source_target_pairs={{0,2},{1,3},{2,0},{3,1},{4,6},{5,7},{6,4},{7,5},{8,10},{9,11},{10,... | collective-permute-start | bytes 1179656 | tf_op jit(solution)/shard_map/ppermute | solution.py:20
  194.9 28.5 %collective-permute-start.36 = (bf16[3,512,128]{2,1,0:T(8,128)(2,1)}, bf16[3,512,128]{2,1,0:T(8,128)(2,1)}, u32[]{:S(2)}, u32[]{:S(2)}) collective-permute-start(bf16[3,512,128]{2,1,0:T(8,128)(2,1)} %get-tuple-element.182.refs_5_), channel_id=1, source_target_pairs={{0,3},{1,2},{2,1},{3,0},{4,7},{5,6},{6,5},{7,4},{8,11},{9,10},{10,... | collective-permute-start | bytes 1179656 | tf_op jit(solution)/shard_map/ppermute | solution.py:20
  196.8 26.5 %collective-permute-start.33 = (bf16[1216,128]{1,0:T(8,128)(2,1)S(1)}, bf16[1216,128]{1,0:T(8,128)(2,1)S(1)}, u32[]{:S(2)}, u32[]{:S(2)}) collective-permute-start(bf16[1216,128]{1,0:T(8,128)(2,1)S(1)} %broadcast_select_fusion.2.refs_1_), channel_id=1, source_target_pairs={{0,4},{4,0},{8,12},{12,8},{16,20},{20,16},{24,28},{28,24},{1,5},{5... | collective-permute-start | bytes 933896 | tf_op jit(solution)/shard_map/ppermute | solution.py:25
  235.3 14.8 %collective-permute-start.40 = (bf16[1024,128]{1,0:T(8,128)(2,1)S(1)}, bf16[1024,128]{1,0:T(8,128)(2,1)S(1)}, u32[]{:S(2)}, u32[]{:S(2)}) collective-permute-start(bf16[1024,128]{1,0:T(8,128)(2,1)S(1)} %get-tuple-element.274), channel_id=1, source_target_pairs={{0,28},{4,0},{8,4},{12,8},{16,12},{20,16},{24,20},{28,24},{1,29},{... | collective-permute-start | bytes 786440 | tf_op jit(solution)/shard_map/ppermute | solution.py:30
  235.7 14.5 %collective-permute-start.41 = (bf16[1024,128]{1,0:T(8,128)(2,1)S(1)}, bf16[1024,128]{1,0:T(8,128)(2,1)S(1)}, u32[]{:S(2)}, u32[]{:S(2)}) collective-permute-start(bf16[1024,128]{1,0:T(8,128)(2,1)S(1)} %get-tuple-element.275), channel_id=1, source_target_pairs={{0,4},{4,8},{8,12},{12,16},{16,20},{20,24},{24,28},{28,0},{1,5},{5... | collective-permute-start | bytes 786440 | tf_op jit(solution)/shard_map/ppermute | solution.py:30
  249.9 15.9 %collective-permute-start.54 = (bf16[608,128]{1,0:T(8,128)(2,1)S(1)}, bf16[608,128]{1,0:T(8,128)(2,1)S(1)}, u32[]{:S(2)}, u32[]{:S(2)}) collective-permute-start(bf16[608,128]{1,0:T(8,128)(2,1)S(1)} %pad_maximum_fusion.14), channel_id=1, source_target_pairs={{0,8},{4,12},{8,0},{12,4},{16,24},{20,28},{24,16},{28,20},{1,9},{5... | collective-permute-start | bytes 466952 | tf_op jit(solution)/shard_map/ppermute | solution.py:25
  261.8 14.9 %collective-permute-start.44 = (bf16[1024,128]{1,0:T(8,128)(2,1)S(1)}, bf16[1024,128]{1,0:T(8,128)(2,1)S(1)}, u32[]{:S(2)}, u32[]{:S(2)}) collective-permute-start(bf16[1024,128]{1,0:T(8,128)(2,1)S(1)} %get-tuple-element.239), channel_id=1, source_target_pairs={{0,1},{1,0},{2,3},{3,2},{4,5},{5,4},{6,7},{7,6},{8,9},{9,8},{10,11... | collective-permute-start | bytes 786440 | tf_op jit(solution)/shard_map/ppermute | solution.py:20
  261.9 14.8 %collective-permute-start.43 = (bf16[1024,128]{1,0:T(8,128)(2,1)S(1)}, bf16[1024,128]{1,0:T(8,128)(2,1)S(1)}, u32[]{:S(2)}, u32[]{:S(2)}) collective-permute-start(bf16[1024,128]{1,0:T(8,128)(2,1)S(1)} %get-tuple-element.240), channel_id=1, source_target_pairs={{0,2},{1,3},{2,0},{3,1},{4,6},{5,7},{6,4},{7,5},{8,10},{9,11},{10,... | collective-permute-start | bytes 786440 | tf_op jit(solution)/shard_map/ppermute | solution.py:20
  (152 other events, 892.7 us)
